TPU v7x, 512 devices: a whole 4x4x16 slice. The times are simulated.
512 devices in a mesh: dp: 128 (over x_hi, y, z), fsdp: 4 (over x_lo, core).
Axes of the slice: x: 4 (x_hi: 2, x_lo: 2; x = x_hi * 2 + x_lo), y: 4, z: 16, core: 2. Of those that a mesh axis runs over, the one named last changes fastest.
Arguments:
- tokens: bfloat16 [65536, 1280], P(('dp', 'fsdp')), may hold values from -3 to 3
- qkv_weight: bfloat16 [3, 1280, 1280], P(None, 'dp', 'fsdp'), may hold values from -1 to 1
- out_weight: bfloat16 [1280, 1280], P('fsdp', 'dp'), may hold values from -0.15625 to 0.15625
- merge_weight: bfloat16 [5120, 1280], P(('dp', 'fsdp')), may hold values from -0.078125 to 0.078125
- ln_gains: float32 [2, 1280], replicated, may hold values from 0.25 to 1.75
- segments: int32 [128, 512], P('dp', 'fsdp'), may hold values from 0 to 2, never falling along the last dimension, each value on 1 to 256 neighbouring positions
- merge_rows: int32 [512, 128], P(('dp', 'fsdp')), may hold values from 0 to 127, each once within a row
- owners: int32 [16384, 1], P(('dp', 'fsdp')), may hold values from 0 to 127; in each aligned block of 32 rows (0 to 31, 32 to 63, ...) at most 2 rows name the same one
Outputs:
- owned: bfloat16 [131072, 1280], P(('dp', 'fsdp'))
Inputs may be any that keep to these rules, and one draw needn't show every extreme that they name: `segments`: within each row segment numbers never fall, every number appears, each request has 1 to 256 tokens and one has exactly 256. `merge_rows`: each row is a permutation of the device's local rows. `owners`: among the 32 merged tokens of one device no owner appears more than 2 times, and in some devices one appears exactly 2 times.
All inputs are finite; a program needn't handle non-finite values.
Results may differ from a plain program's by a relative error of at most 0.02.
Values may be sent and summed in bfloat16 or wider, within the bound.
A program may use at most 64 MiB of HBM per device.

v0:
```python
import math

import jax
import jax.numpy as jnp
from jax import lax
from jax.sharding import PartitionSpec as P

HD = 80


epsilon = 1e-06


def normalize(values_in, gain_row):
    widened = values_in.astype(jnp.float32)
    centered = widened - jnp.mean(widened, axis=1, keepdims=True)
    variance = jnp.mean(centered * centered, axis=1, keepdims=True)
    return (centered * lax.rsqrt(variance + epsilon) * gain_row).astype(jnp.bfloat16)


def attend(queries, keys_all, values_all, seg_rows, seg_cols):
    factor = 1.0 / math.sqrt(HD)
    allowed = seg_rows[:, None] == seg_cols[None, :]
    pieces = []
    for head_index in range(queries.shape[1] // HD):
        first_col = head_index * HD
        last_col = first_col + HD
        scores = (
            lax.dot_general(
                queries[:, first_col:last_col],
                keys_all[:, first_col:last_col],
                (((1,), (1,)), ((), ())),
                preferred_element_type=jnp.float32,
            )
            * factor
        )
        masked = jnp.where(allowed, scores, -jnp.inf)
        highest = jnp.max(masked, axis=1, keepdims=True)
        weights = jnp.exp(masked - highest)
        totals = jnp.sum(weights, axis=1, keepdims=True)
        head_out = jnp.dot(
            weights.astype(jnp.bfloat16),
            values_all[:, first_col:last_col],
            preferred_element_type=jnp.float32,
        )
        pieces.append(head_out / totals)
    return jnp.concatenate(pieces, axis=1).astype(jnp.bfloat16)


def per_device(
    tokens, qkv_weight, out_weight, merge_weight, ln_gains, segments, merge_rows, owners
):
    n_dp = lax.axis_size("dp")
    n_fsdp = lax.axis_size("fsdp")
    qkv_mine = lax.all_gather(qkv_weight, "dp", axis=1, tiled=True)
    out_mine = lax.all_gather(out_weight, "dp", axis=1, tiled=True)
    normed = normalize(tokens, ln_gains[0])
    group_normed, group_segs = (
        lax.all_gather(normed, "fsdp", axis=0, tiled=True),
        lax.all_gather(segments, "fsdp", axis=1, tiled=True),
    )
    queries = jnp.dot(group_normed, qkv_mine[0], preferred_element_type=jnp.float32).astype(
        jnp.bfloat16
    )
    keys_all = jnp.dot(group_normed, qkv_mine[1], preferred_element_type=jnp.float32).astype(
        jnp.bfloat16
    )
    values_all = jnp.dot(group_normed, qkv_mine[2], preferred_element_type=jnp.float32).astype(
        jnp.bfloat16
    )
    attended_mine = attend(queries, keys_all, values_all, group_segs[0], group_segs[0])
    attended_local = lax.all_to_all(attended_mine, "fsdp", split_axis=0, concat_axis=1, tiled=True)
    out_full = lax.all_gather(out_mine, "fsdp", axis=0, tiled=True)
    update = jnp.dot(attended_local, out_full, preferred_element_type=jnp.float32)
    layer_out = (tokens.astype(jnp.float32) + update).astype(jnp.bfloat16)
    merge_in = normalize(layer_out, ln_gains[1])
    merge_count = tokens.shape[0] // 4
    stacked = jnp.take(merge_in, merge_rows[0], axis=0).reshape(merge_count, 4 * merge_in.shape[1])
    slice_rows = merge_weight.shape[0]
    part_rows = lax.all_gather(merge_weight, "dp", axis=0, tiled=True)
    blocks = stacked.reshape(merge_count, n_dp, n_fsdp * slice_rows)
    received = lax.all_to_all(blocks, "fsdp", split_axis=2, concat_axis=0, tiled=True)
    gathered_inputs = received.reshape(n_fsdp * merge_count, n_dp * slice_rows)
    merged = lax.psum_scatter(
        jnp.dot(gathered_inputs, part_rows, preferred_element_type=jnp.float32).astype(
            jnp.bfloat16
        ),
        "fsdp",
        scatter_dimension=0,
        tiled=True,
    )
    capacity = max(2, (2 * merge_count + n_dp - 1) // n_dp)
    targets = owners[:, 0]
    onehot = (targets[:, None] == jnp.arange(n_dp, dtype=jnp.int32)[None, :]).astype(jnp.int32)
    earlier = jnp.cumsum(onehot, axis=0) - onehot
    position = jnp.sum(earlier * onehot, axis=1)
    slot_index = targets * capacity + position
    placing = (jnp.arange(n_dp * capacity, dtype=jnp.int32)[:, None] == slot_index[None, :]).astype(
        jnp.bfloat16
    )
    packed = jnp.dot(placing, merged, preferred_element_type=jnp.float32).astype(jnp.bfloat16)
    packed = packed.reshape(n_dp, capacity, merged.shape[1])
    arrived = lax.all_to_all(packed, "dp", split_axis=0, concat_axis=0, tiled=True)
    return arrived.reshape(n_dp * capacity, merged.shape[1])


def solution(mesh):
    return jax.shard_map(
        per_device,
        mesh=mesh,
        in_specs=(
            P(("dp", "fsdp"), None),
            P(None, "dp", "fsdp"),
            P("fsdp", "dp"),
            P(("dp", "fsdp"), None),
            P(),
            P("dp", "fsdp"),
            P(("dp", "fsdp"), None),
            P(("dp", "fsdp"), None),
        ),
        out_specs=P(("dp", "fsdp"), None),
        check_vma=False,
    )
```

profile of v0, /device:TPU:24, one launch (start us, length us, event | category | flops | bytes accessed | tf_op | source)
XLA Modules:
  0.0 749.1 jit_solution(5897725297791308447)
XLA Ops:
  6.5 0.7 all-gather.9.cloned.1.call-update
  7.3 0.8 slice_reduce_fusion
  8.1 1.1 convert_reduce_fusion
  9.2 1.2 fusion.23
  10.4 1.9 fusion.25
  12.4 323.9 %all-gather = bf16[128,10,320]{2,1,0:T(8,128)(2,1)S(1)} all-gather(bf16[1,10,320]{2,1,0:T(8,128)(2,1)} %bitcast.57), channel_id=1, replica_groups=mesh['dp'=128,'fsdp'=4] {'dp'}, dimensions={0}, use_global_device_ids=true | all-gather | bytes 825600 | tf_op jit(solution)/shard_map/all_gather | solution.py:56
  337.0 1.3 copy.23
  338.9 5.0 all_gather.18
  344.4 0.6 reduce.7
  345.4 10.5 %fusion.49 = (bf16[1,1280,320]{2,0,1:T(2,128)(2,1)S(1)}, bf16[1,1280,320]{2,0,1:T(2,128)(2,1)}, bf16[1,1280,320]{2,0,1:T(2,128)(2,1)}) fusion(bf16[3,1280,320]{2,0,1:T(4,128)(2,1)} %all-gather.9.cloned.1.call-done), kind=kLoop, calls=%fused_computation.92 | loop fusion | bytes 4915200 | tf_op jit(solution)/shard_map/slice | solution.py:68
  355.9 4.9 copy.28
  360.8 4.9 copy.27
  365.6 2.8 copy.26
  368.4 2.3 convolution_convert_fusion.3
  375.6 0.7 pad_maximum_fusion
  376.3 3.5 all-to-all-start
  380.1 38.7 %all-gather.11.cloned.1.call-done = bf16[1280,1280]{1,0:T(8,128)(2,1)} async-done(((bf16[320,1280]{1,0:T(8,128)(2,1)}), bf16[1280,1280]{1,0:T(8,128)(2,1)}) %all-gather.11.cloned.1.call-update) | async-done | bytes 3276816 | tf_op jit(solution)/shard_map/all_gather | solution.py:73
  418.8 2.6 fusion.54
  421.8 0.9 gather_fusion
  422.7 1.9 gather.7
  424.6 0.7 broadcast_select_fusion
  425.3 0.6 copy.24
  426.0 9.1 %all_to_all.36 = bf16[32,128,40]{1,0,2:T(8,128)(2,1)S(1)} all-to-all(bf16[32,128,40]{1,0,2:T(8,128)(2,1)S(1)} %copy.24), channel_id=1, replica_groups=mesh['dp'=128,'fsdp'=4] {'fsdp'}, dimensions={2} | all-to-all | bytes 655360 | tf_op jit(solution)/shard_map/all_to_all | solution.py:82
  435.1 0.8 copy.25
  435.9 1.4 reshape.100
  437.2 219.1 %all-gather.13.cloned.1.call-done = bf16[128,10,1280]{2,1,0:T(8,128)(2,1)} async-done(((bf16[1,10,1280]{2,1,0:T(8,128)(2,1)}), bf16[128,10,1280]{2,1,0:T(8,128)(2,1)}) %all-gather.13.cloned.1.call-update) | async-done | bytes 3276816 | tf_op jit(solution)/shard_map/all_gather | solution.py:80
  656.3 5.3 reshape.114
  661.6 2.3 convolution_convert_fusion.1
  664.3 19.3 %reduce-scatter.2.cloned.1.call-done = bf16[32,1280]{1,0:T(8,128)(2,1)} async-done(((bf16[128,1280]{1,0:T(8,128)(2,1)}), bf16[32,1280]{1,0:T(8,128)(2,1)}) %reduce-scatter.2.cloned.1.call-update) | async-done | bytes 81936 | tf_op jit(solution)/shard_map/reduce_scatter | solution.py:84
  683.6 1.2 convolution_convert_fusion
  685.1 56.4 %all_to_all.37 = bf16[128,2,1280]{2,1,0:T(2,128)(2,1)S(1)} all-to-all(bf16[128,2,1280]{2,1,0:T(2,128)(2,1)S(1)} %reshape.101), channel_id=1, replica_groups=mesh['dp'=128,'fsdp'=4] {'dp'}, dimensions={0} | all-to-all | bytes 1310720 | tf_op jit(solution)/shard_map/all_to_all | solution.py:103
  741.5 1.1 reshape.102
  (59 shorter events, 8.2 us)
Async XLA Ops:
  6.5 338.9 %all-gather.9.cloned.1.call-start = ((), (), s32[]{:S(2)}) async-start(), calls=%async_computation.5 | async-start | bytes 3962880 | tf_op jit(solution)/shard_map/all_gather | solution.py:55
  7.3 361.2 %all-gather.7.cloned.1.call-start = ((), (), s32[]{:S(2)}) async-start(), calls=%async_computation.4 | async-start | bytes 1638400 | tf_op jit(solution)/shard_map/all_gather | solution.py:59
  12.4 406.4 %all-gather.11.cloned.1.call-start = ((), (), s32[]{:S(2)}) async-start(), calls=%async_computation.6 | async-start | bytes 4096000 | tf_op jit(solution)/shard_map/all_gather | solution.py:73
  336.9 1.9 copy-start.3
  336.9 7.5 copy-start.5
  338.3 318.1 %all-gather.13.cloned.1.call-start = ((), (), s32[]{:S(2)}) async-start(), calls=%async_computation.8 | async-start | bytes 5283840 | tf_op jit(solution)/shard_map/all_gather | solution.py:80
  368.4 2.4 copy-start.1
  368.4 2.3 copy-start.4
  374.9 43.9 %copy-start = (bf16[128,1280]{1,0:T(8,128)(2,1)S(1)}, bf16[128,1280]{1,0:T(8,128)(2,1)}, u32[]{:S(2)}) copy-start(bf16[128,1280]{1,0:T(8,128)(2,1)} %param.8) | copy-start | bytes 983044
  376.3 42.4 %all-to-all-start = ((bf16[4,128,320]{1,2,0:T(8,128)(2,1)}), bf16[4,128,320]{1,2,0:T(8,128)(2,1)S(1)}, u32[]{:S(2)}, u32[]{:S(2)}) async-start(bf16[4,128,320]{1,2,0:T(8,128)(2,1)} %pad_maximum_fusion), calls=%async_computation | async-start | bytes 655360 | tf_op jit(solution)/shard_map/all_to_all | solution.py:72
  379.8 303.8 %reduce-scatter.2.cloned.1.call-start = ((), (), s32[]{:S(2)}) async-start(), calls=%async_computation.7 | async-start | bytes 409600 | tf_op jit(solution)/shard_map/reduce_scatter | solution.py:84
  661.6 2.4 copy-start.2
Sparse Core Ops, SparseCore 0:
  11.8 227.2 all-gather.8
  241.3 25.4 all-gather.6
  338.4 80.3 all-gather.10
  423.0 233.2 all-gather.12
  664.1 19.4 reduce-scatter.1
where the time goes:
time: 752 us; the launch traced here: 749 us
  blocking collectives  394 us (52%)
  waiting for transfers between devices  278 us (37%)
  local copies, waits for them, and re-layouts  38.7 us (5%)
  between operations  13.5 us (2%)
  matrix products  12.4 us (2%)
  other arithmetic  7.87 us (1%)
    all_gather x1, blocking collectives, per_device(): out_mine = lax.all_gather(out_weight, 'dp', axis=1, tiled=True)  324 us
    all_gather x1, waiting for transfers between devices, per_device(): part_rows = lax.all_gather(merge_weight, 'dp', axis=0, tiled=True)  219 us
    all_to_all x1, blocking collectives, per_device(): lax.all_to_all(packed, 'dp', split_axis=0, concat_axis=0, tiled=True)  56.4 us
    all_gather x1, waiting for transfers between devices, per_device(): out_full = lax.all_gather(out_mine, 'fsdp', axis=0, tiled=True)  38.7 us
    unnamed x19, local copies, waits for them, and re-layouts  20.2 us
    reduce_scatter x1, waiting for transfers between devices, per_device(): lax.psum_scatter(jnp.dot(gathered_inputs, part_rows, preferred_element_ty...  19.3 us
  transfers between devices with their start and end apart: 6, of which 3 were waited for; matrix products, arithmetic and copies ran while one was open for 7% of the time, Pallas kernels for 0%

commit v1 on v0

--- a/solution.py
+++ b/solution.py
@@ -1,11 +1,189 @@
+import functools
 import math
 
 import jax
 import jax.numpy as jnp
 from jax import lax
+from jax.experimental import pallas as pl
+from jax.experimental.pallas import tpu as pltpu
 from jax.sharding import PartitionSpec as P
 
 HD = 80
+NZ = 16
+NY = 4
+CH = 5
+CW = 256
+MESH = pl.DeviceIdType.MESH
+
+
+def coords():
+    dp = lax.axis_index("dp")
+    fs = lax.axis_index("fsdp")
+    return dp // 64, (dp // 16) % 4, dp % 16, fs
+
+
+def deliver_kernel(
+    merged_ref, slots_ref, out_ref, rows, keys, picked, landed, zs_send, zs_recv, ks_send, ks_recv, p_send, p_recv
+):
+    xh, y, z, fs = coords()
+    plane = xh * 64 + y * 16
+    mine = xh * 4 + y
+    up = plane + (z + 1) % NZ
+    down = plane + (z + NZ - 1) % NZ
+
+    barrier = pltpu.get_barrier_semaphore()
+    for peer in (up, down):
+        pl.semaphore_signal(barrier, inc=1, device_id=(peer, fs), device_id_type=MESH)
+    for step in range(1, 8):
+        other = (mine + step) % 8
+        pl.semaphore_signal(barrier, inc=1, device_id=(other * 16 + z, fs), device_id_type=MESH)
+    for c in range(CH):
+        rows[c, pl.ds(pl.multiple_of(z * 32, 32), 32), :] = merged_ref[:, c * CW : (c + 1) * CW]
+    keys[z] = slots_ref[...]
+    pl.semaphore_wait(barrier, 9)
+
+    def key_copy(way, step):
+        src = (z + NZ - (step - 1)) % NZ if way == 0 else (z + step - 1) % NZ
+        return pltpu.make_async_remote_copy(
+            src_ref=keys.at[src],
+            dst_ref=keys.at[src],
+            send_sem=ks_send.at[way, step - 1],
+            recv_sem=ks_recv.at[way, step - 1],
+            device_id=(up if way == 0 else down, fs),
+            device_id_type=MESH,
+        )
+
+    def row_copy(c, way, step):
+        src = (z + NZ - (step - 1)) % NZ if way == 0 else (z + step - 1) % NZ
+        piece = rows.at[c, pl.ds(pl.multiple_of(src * 32, 32), 32), :]
+        return pltpu.make_async_remote_copy(
+            src_ref=piece,
+            dst_ref=piece,
+            send_sem=zs_send.at[c, way, step - 1],
+            recv_sem=zs_recv.at[c, way, step - 1],
+            device_id=(up if way == 0 else down, fs),
+            device_id_type=MESH,
+        )
+
+    def row_arrival(c, way, step):
+        src = (z + NZ - step) % NZ if way == 0 else (z + step) % NZ
+        piece = rows.at[c, pl.ds(pl.multiple_of(src * 32, 32), 32), :]
+        return pltpu.make_async_remote_copy(
+            src_ref=piece,
+            dst_ref=piece,
+            send_sem=zs_send.at[c, way, step - 1],
+            recv_sem=zs_recv.at[c, way, step - 1],
+            device_id=(up if way == 0 else down, fs),
+            device_id_type=MESH,
+        )
+
+    def key_arrival(way, step):
+        src = (z + NZ - step) % NZ if way == 0 else (z + step) % NZ
+        return pltpu.make_async_remote_copy(
+            src_ref=keys.at[src],
+            dst_ref=keys.at[src],
+            send_sem=ks_send.at[way, step - 1],
+            recv_sem=ks_recv.at[way, step - 1],
+            device_id=(up if way == 0 else down, fs),
+            device_id_type=MESH,
+        )
+
+    def plane_copy(c, step):
+        other = (mine + step) % 8
+        return pltpu.make_async_remote_copy(
+            src_ref=picked.at[c, pl.ds(pl.multiple_of(other * 32, 32), 32), :],
+            dst_ref=landed.at[c, pl.ds(pl.multiple_of(mine * 32, 32), 32), :],
+            send_sem=p_send.at[c, step - 1],
+            recv_sem=p_recv.at[c, step - 1],
+            device_id=(other * 16 + z, fs),
+            device_id_type=MESH,
+        )
+
+    def plane_arrival(c, step):
+        other = (mine + 8 - step) % 8
+        return pltpu.make_async_remote_copy(
+            src_ref=picked.at[c, pl.ds(pl.multiple_of(other * 32, 32), 32), :],
+            dst_ref=landed.at[c, pl.ds(pl.multiple_of(other * 32, 32), 32), :],
+            send_sem=p_send.at[c, step - 1],
+            recv_sem=p_recv.at[c, step - 1],
+            device_id=(other * 16 + z, fs),
+            device_id_type=MESH,
+        )
+
+    last = (8, 7)
+    key_copy(0, 1).start()
+    key_copy(1, 1).start()
+    for c in range(CH):
+        for way in range(2):
+            row_copy(c, way, 1).start()
+    chosen = None
+    for wave in range(1, 8 + CH):
+        if wave <= 8:
+            for way in range(2):
+                if wave <= last[way]:
+                    key_arrival(way, wave).wait_recv()
+                    if wave < last[way]:
+                        key_copy(way, wave + 1).start()
+        for c in range(CH):
+            step = wave - c
+            for way in range(2):
+                if 1 <= step <= last[way]:
+                    row_arrival(c, way, step).wait_recv()
+                    if step < last[way]:
+                        row_copy(c, way, step + 1).start()
+        c = wave - 8
+        if c >= 0:
+            if chosen is None:
+                pieces = [
+                    keys[4 * q, 0:1, :] + keys[4 * q + 1, 0:1, :] + keys[4 * q + 2, 0:1, :] + keys[4 * q + 3, 0:1, :]
+                    for q in range(4)
+                ]
+                row_key = jnp.concatenate(pieces, axis=1)
+                place = lax.broadcasted_iota(jnp.int32, (256, 512), 0)
+                column = lax.broadcasted_iota(jnp.int32, (256, 512), 1)
+                wanted = (place & 224) + 2 * z + (place & 1) + 1
+                same = ((place >> 1) & 15) == (column >> 5)
+                chosen = jnp.where(same & (row_key == wanted), 1.0, 0.0).astype(jnp.bfloat16)
+            picked[c] = jnp.dot(chosen, rows[c], preferred_element_type=jnp.float32).astype(jnp.bfloat16)
+            for step in range(1, 8):
+                plane_copy(c, step).start()
+    for c in range(CH):
+        own = pl.ds(pl.multiple_of(mine * 32, 32), 32)
+        landed[c, own, :] = picked[c, own, :]
+        for step in range(1, 8):
+            plane_arrival(c, step).wait_recv()
+        out_ref[:, c * CW : (c + 1) * CW] = landed[c]
+    for way in range(2):
+        for step in range(1, last[way] + 1):
+            key_copy(way, step).wait_send()
+            for c in range(CH):
+                row_copy(c, way, step).wait_send()
+    for c in range(CH):
+        for step in range(1, 8):
+            plane_copy(c, step).wait_send()
+
+
+def deliver(merged, slots):
+    width = merged.shape[1]
+    return pl.pallas_call(
+        deliver_kernel,
+        out_shape=jax.ShapeDtypeStruct((256, width), jnp.bfloat16),
+        in_specs=[pl.BlockSpec(memory_space=pltpu.VMEM)] * 2,
+        out_specs=pl.BlockSpec(memory_space=pltpu.VMEM),
+        scratch_shapes=[
+            pltpu.VMEM((CH, 512, CW), jnp.bfloat16),
+            pltpu.VMEM((NZ, 8, 128), jnp.int32),
+            pltpu.VMEM((CH, 256, CW), jnp.bfloat16),
+            pltpu.VMEM((CH, 256, CW), jnp.bfloat16),
+            pltpu.SemaphoreType.DMA((CH, 2, 8)),
+            pltpu.SemaphoreType.DMA((CH, 2, 8)),
+            pltpu.SemaphoreType.DMA((2, 8)),
+            pltpu.SemaphoreType.DMA((2, 8)),
+            pltpu.SemaphoreType.DMA((CH, 7)),
+            pltpu.SemaphoreType.DMA((CH, 7)),
+        ],
+        compiler_params=pltpu.CompilerParams(collective_id=0, has_side_effects=True),
+    )(merged, slots)
 
 
 epsilon = 1e-06
@@ -89,19 +267,14 @@
         scatter_dimension=0,
         tiled=True,
     )
-    capacity = max(2, (2 * merge_count + n_dp - 1) // n_dp)
     targets = owners[:, 0]
     onehot = (targets[:, None] == jnp.arange(n_dp, dtype=jnp.int32)[None, :]).astype(jnp.int32)
     earlier = jnp.cumsum(onehot, axis=0) - onehot
     position = jnp.sum(earlier * onehot, axis=1)
-    slot_index = targets * capacity + position
-    placing = (jnp.arange(n_dp * capacity, dtype=jnp.int32)[:, None] == slot_index[None, :]).astype(
-        jnp.bfloat16
-    )
-    packed = jnp.dot(placing, merged, preferred_element_type=jnp.float32).astype(jnp.bfloat16)
-    packed = packed.reshape(n_dp, capacity, merged.shape[1])
-    arrived = lax.all_to_all(packed, "dp", split_axis=0, concat_axis=0, tiled=True)
-    return arrived.reshape(n_dp * capacity, merged.shape[1])
+    slot_row = targets * 2 + position + 1
+    quarter = lax.axis_index("dp") % 4
+    spread = jnp.where(jnp.arange(4)[:, None] == quarter, slot_row[None, :], 0).reshape(1, 128)
+    return deliver(merged, jnp.broadcast_to(spread, (8, 128)))
 
 
 def solution(mesh):

time: 752 us -> 751 us (level)
  blocking collectives: 394 us -> 329 us
  Pallas kernels: 0 us -> 57.1 us
    all_to_all x2 -> x0, blocking collectives: 65.5 us -> none  [the longest x1 56.4 us: per_device(): lax.all_to_all(packed, 'dp', split_axis=0, concat_axis=0, tiled=True)]
    pallas_call x0 -> x1, Pallas kernels: none -> 57.1 us  [deliver(): pl.pallas_call(deliver_kernel, out_shape=jax.ShapeDtypeStruct((256, width...]
    unnamed x19 -> x20, local copies, waits for them, and re-layouts: 20.2 us -> 22.2 us
  transfers between devices with their start and end apart: 6 -> 7, of which waited for: 3 -> 4; matrix products, arithmetic and copies ran while one was open for 7% -> 7% of each run, Pallas kernels for 0% -> 0%
where the time goes in v1:
time: 751 us; the launch traced here: 750 us
  blocking collectives  329 us (44%)
  waiting for transfers between devices  283 us (38%)
  Pallas kernels  57.1 us (8%)
  local copies, waits for them, and re-layouts  40.8 us (5%)
  between operations  13.5 us (2%)
  matrix products  11.2 us (1%)
  other arithmetic  7.95 us (1%)
    all_gather x1, blocking collectives, per_device(): out_mine = lax.all_gather(out_weight, 'dp', axis=1, tiled=True)  324 us
    all_gather x1, waiting for transfers between devices, per_device(): part_rows = lax.all_gather(merge_weight, 'dp', axis=0, tiled=True)  217 us
    pallas_call x1, Pallas kernels, deliver(): pl.pallas_call(deliver_kernel, out_shape=jax.ShapeDtypeStruct((256, width...  57.1 us
    all_gather x1, waiting for transfers between devices, per_device(): out_full = lax.all_gather(out_mine, 'fsdp', axis=0, tiled=True)  38.8 us
    unnamed x20, local copies, waits for them, and re-layouts  22.2 us
    reduce_scatter x1, waiting for transfers between devices, per_device(): lax.psum_scatter(jnp.dot(gathered_inputs, part_rows, preferred_element_ty...  19.3 us
  transfers between devices with their start and end apart: 7, of which 4 were waited for; matrix products, arithmetic and copies ran while one was open for 7% of the time, Pallas kernels for 0%

profile of v1, /device:TPU:24, one launch (start us, length us, event | category | flops | bytes accessed | tf_op | source)
XLA Modules:
  0.0 749.8 jit_solution(16044634643284813129)
XLA Ops:
  6.5 0.7 all-gather.9.cloned.1.call-update
  7.3 0.8 slice_reduce_fusion
  8.1 1.1 convert_reduce_fusion
  9.2 1.2 fusion.23
  10.4 1.9 fusion.25
  12.4 323.9 %all-gather = bf16[128,10,320]{2,1,0:T(8,128)(2,1)S(1)} all-gather(bf16[1,10,320]{2,1,0:T(8,128)(2,1)} %bitcast.56), channel_id=1, replica_groups=mesh['dp'=128,'fsdp'=4] {'dp'}, dimensions={0}, use_global_device_ids=true | all-gather | bytes 825600 | tf_op jit(solution)/shard_map/all_gather | solution.py:234
  337.0 1.3 copy.23
  338.9 5.0 all_gather.18
  344.4 0.6 reduce.7
  345.4 10.5 %fusion.48 = (bf16[1,1280,320]{2,0,1:T(2,128)(2,1)S(1)}, bf16[1,1280,320]{2,0,1:T(2,128)(2,1)}, bf16[1,1280,320]{2,0,1:T(2,128)(2,1)}) fusion(bf16[3,1280,320]{2,0,1:T(4,128)(2,1)} %all-gather.9.cloned.1.call-done), kind=kLoop, calls=%fused_computation.91 | loop fusion | bytes 4915200 | tf_op jit(solution)/shard_map/slice | solution.py:246
  355.9 4.9 copy.28
  360.8 4.9 copy.27
  365.6 2.8 copy.26
  368.4 2.3 convolution_convert_fusion.2
  375.6 0.7 pad_maximum_fusion
  376.3 3.6 all-to-all-start
  380.0 38.8 %all-gather.11.cloned.1.call-done = bf16[1280,1280]{1,0:T(8,128)(2,1)} async-done(((bf16[320,1280]{1,0:T(8,128)(2,1)}), bf16[1280,1280]{1,0:T(8,128)(2,1)}) %all-gather.11.cloned.1.call-update) | async-done | bytes 3276816 | tf_op jit(solution)/shard_map/all_gather | solution.py:251
  418.8 2.6 fusion.53
  421.8 0.9 gather_fusion
  422.7 1.9 gather.7
  424.6 0.7 broadcast_select_fusion
  425.4 1.3 copy.24
  426.7 3.5 all-to-all-start.1
  430.3 6.5 all-to-all-done.1
  436.8 0.8 copy.25
  437.6 1.4 reshape.116
  439.0 217.3 %all-gather.13.cloned.1.call-done = bf16[128,10,1280]{2,1,0:T(8,128)(2,1)} async-done(((bf16[1,10,1280]{2,1,0:T(8,128)(2,1)}), bf16[128,10,1280]{2,1,0:T(8,128)(2,1)}) %all-gather.13.cloned.1.call-update) | async-done | bytes 3276816 | tf_op jit(solution)/shard_map/all_gather | solution.py:258
  656.3 5.3 reshape.128
  661.6 2.3 convolution_convert_fusion
  664.3 19.3 %reduce-scatter.2.cloned.1.call-done.merged_ref = bf16[32,1280]{1,0:T(8,128)(2,1)} async-done(((bf16[128,1280]{1,0:T(8,128)(2,1)}), bf16[32,1280]{1,0:T(8,128)(2,1)}) %reduce-scatter.2.cloned.1.call-update) | async-done | bytes 81936 | tf_op jit(solution)/shard_map/reduce_scatter | solution.py:262
  684.2 57.1 %shard_map.82 = bf16[256,1280]{1,0:T(8,128)(2,1)} custom-call(bf16[32,1280]{1,0:T(8,128)(2,1)} %reduce-scatter.2.cloned.1.call-done.merged_ref, s32[8,128]{1,0:T(8,128)} %broadcast_in_dim.69.slots_ref), custom_call_target="tpu_custom_call" | custom-call | tf_op jit(solution)/shard_map/pallas_call | solution.py:168
  741.3 2.0 copy.38
  (62 shorter events, 8.5 us)
Async XLA Ops:
  6.5 338.9 %all-gather.9.cloned.1.call-start = ((), (), s32[]{:S(2)}) async-start(), calls=%async_computation.4 | async-start | bytes 3962880 | tf_op jit(solution)/shard_map/all_gather | solution.py:233
  7.3 361.2 %all-gather.7.cloned.1.call-start = ((), (), s32[]{:S(2)}) async-start(), calls=%async_computation.3 | async-start | bytes 1638400 | tf_op jit(solution)/shard_map/all_gather | solution.py:237
  12.4 406.4 %all-gather.11.cloned.1.call-start = ((), (), s32[]{:S(2)}) async-start(), calls=%async_computation.5 | async-start | bytes 4096000 | tf_op jit(solution)/shard_map/all_gather | solution.py:251
  336.9 1.9 copy-start.3
  336.9 7.5 copy-start.5
  338.3 318.1 %all-gather.13.cloned.1.call-start = ((), (), s32[]{:S(2)}) async-start(), calls=%async_computation.7 | async-start | bytes 5283840 | tf_op jit(solution)/shard_map/all_gather | solution.py:258
  368.4 2.4 copy-start.1
  368.4 2.3 copy-start.4
  374.9 43.9 %copy-start = (bf16[128,1280]{1,0:T(8,128)(2,1)S(1)}, bf16[128,1280]{1,0:T(8,128)(2,1)}, u32[]{:S(2)}) copy-start(bf16[128,1280]{1,0:T(8,128)(2,1)} %param.8) | copy-start | bytes 983044
  376.3 42.4 %all-to-all-start = ((bf16[4,128,320]{1,2,0:T(8,128)(2,1)}), bf16[4,128,320]{1,2,0:T(8,128)(2,1)S(1)}, u32[]{:S(2)}, u32[]{:S(2)}) async-start(bf16[4,128,320]{1,2,0:T(8,128)(2,1)} %pad_maximum_fusion), calls=%async_computation | async-start | bytes 655360 | tf_op jit(solution)/shard_map/all_to_all | solution.py:250
  424.6 5.6 copy-start.2
  426.7 10.2 %all-to-all-start.1 = ((bf16[32,128,40]{1,0,2:T(8,128)(2,1)}), bf16[32,128,40]{1,0,2:T(8,128)(2,1)S(1)}, u32[]{:S(2)}, u32[]{:S(2)}) async-start(bf16[32,128,40]{1,0,2:T(8,128)(2,1)} %copy.24), calls=%async_computation.1 | async-start | bytes 655360 | tf_op jit(solution)/shard_map/all_to_all | solution.py:260
  430.1 253.5 %reduce-scatter.2.cloned.1.call-start = ((), (), s32[]{:S(2)}) async-start(), calls=%async_computation.6 | async-start | bytes 409600 | tf_op jit(solution)/shard_map/reduce_scatter | solution.py:262
Sparse Core Ops, SparseCore 0:
  11.8 227.2 all-gather.8
  241.3 25.4 all-gather.6
  338.4 80.3 all-gather.10
  423.0 233.2 all-gather.12
  664.1 19.4 reduce-scatter.1

commit v2 on v1

v2 whole, which is shorter than its diff:
```python
import math

import jax
import jax.numpy as jnp
from jax import lax
from jax.experimental import pallas as pl
from jax.experimental.pallas import tpu as pltpu
from jax.sharding import Mesh
from jax.sharding import PartitionSpec as P

HD = 80
NZ = 16
NY = 4
MESH = pl.DeviceIdType.MESH
XG = ("xh", "fsdp")
epsilon = 1e-06


def coords():
    yz = lax.axis_index("yz")
    return lax.axis_index("xh"), yz // NZ, yz % NZ, lax.axis_index("fsdp")


def rows_of(place, n):
    return pl.ds(pl.multiple_of(place * n, n), n)


def gather_kernel(
    q_in, o_in, m_in, normed_in, seg_in, wq, wo, wm, normed_all, seg_all,
    q_box, o_box, m_box, q_send, q_recv, o_send, o_recv, m_send, m_recv, n_send, n_recv, g_send, g_recv,
    zq_send, zq_recv, zo_send, zo_recv, zm_send, zm_recv, s_send, s_recv,
):
    xh, y, z, fs = coords()
    core = fs % 2
    xlo = fs // 2
    mine = xh * 4 + y
    member = xh * 4 + fs
    up, down = (z + 1) % NZ, (z + NZ - 1) % NZ

    def dev(xh_, y_, z_, fs_):
        return (xh_, y_ * NZ + z_, fs_)

    barrier = pltpu.get_barrier_semaphore()
    for peer in (up, down):
        pl.semaphore_signal(barrier, inc=1, device_id=dev(xh, y, peer, fs), device_id_type=MESH)
    for dx in range(2):
        for dy in range(4):
            for df in range(4):
                if dx or dy or df:
                    there = dev((xh + dx) % 2, (y + dy) % 4, z, (fs + df) % 4)
                    pl.semaphore_signal(barrier, inc=1, device_id=there, device_id_type=MESH)
    pl.semaphore_wait(barrier, 33)

    def copy(src, dst, ssem, rsem, where):
        return pltpu.make_async_remote_copy(
            src_ref=src, dst_ref=dst, send_sem=ssem, recv_sem=rsem, device_id=where, device_id_type=MESH
        )

    def q_copy(step):
        dx, dy = step // 4, step % 4
        oxh, oy = (xh + dx) % 2, (y + dy) % 4
        return copy(q_in.at[oxh], q_box.at[mine], q_send.at[step], q_recv.at[step], dev(oxh, oy, z, fs))

    def q_arrival(step):
        dx, dy = step // 4, step % 4
        oxh, oy = (xh + dx) % 2, (y + 4 - dy) % 4
        return copy(q_in.at[xh], q_box.at[oxh * 4 + oy], q_send.at[step], q_recv.at[step], dev(oxh, oy, z, fs))

    for step in range(1, 8):
        q_copy(step).start()
    q_box[mine] = q_in[xh]

    o_steps = [(dx, dl, dy) for dx in range(2) for dl in range(2) for dy in range(4)]

    def o_slot(c, d):
        return o_box.at[c, d]

    def o_copy(k):
        dx, dl, dy = o_steps[k]
        oxh, olo, oy = (xh + dx) % 2, (xlo + dl) % 2, (y + dy) % 4
        return copy(o_in, o_slot(core, mine), o_send.at[k], o_recv.at[core, k], dev(oxh, oy, z, olo * 2 + xlo))

    def o_arrival(c, k):
        dx, dl, dy = o_steps[k]
        oxh, oy = (xh + dx) % 2, (y + 4 - dy) % 4
        return copy(o_in, o_slot(c, oxh * 4 + oy), o_send.at[k], o_recv.at[c, k], dev(oxh, oy, z, core * 2 + c))

    def o_remote(k):
        dx, dl, dy = o_steps[k]
        if dx or dy:
            return None
        return (xlo + dl) % 2 * 2 + xlo != fs

    for k in range(16):
        cond = o_remote(k)
        if cond is None:
            o_copy(k).start()
        else:
            @pl.when(cond)
            def _():
                o_copy(k).start()

    @pl.when(xlo == core)
    def _():
        o_box[core, mine] = o_in[...]

    def m_copy(dy):
        return copy(m_in, m_box.at[fs], m_send.at[dy], m_recv.at[fs], dev(xh, (y + dy) % 4, z, y))

    def m_arrival(j):
        return copy(m_in, m_box.at[j], m_send.at[0], m_recv.at[j], dev(xh, fs, z, j))

    for dy in range(1, 4):
        m_copy(dy).start()

    @pl.when(fs != y)
    def _():
        m_copy(0).start()

    @pl.when(fs == y)
    def _():
        m_box[fs] = m_in[...]

    def n_pair(step, to):
        dx, df = step // 4, step % 4
        oxh = (xh + dx) % 2
        ofs = (fs + df) % 4 if to else (fs + 4 - df) % 4
        slot = member if to else oxh * 4 + ofs
        there = dev(oxh, y, z, ofs)
        return (
            copy(normed_in, normed_all.at[slot], n_send.at[step], n_recv.at[step], there),
            copy(seg_in, seg_all.at[slot], g_send.at[step], g_recv.at[step], there),
        )

    for step in range(1, 8):
        for one in n_pair(step, True):
            one.start()
    normed_all[member] = normed_in[...]
    seg_all[member] = seg_in[...]

    def ten(count, depth):
        place = lax.broadcasted_iota(jnp.int32, (count, depth), 0)
        column = lax.broadcasted_iota(jnp.int32, (count, depth), 1)
        tens = (place * 52429) >> 19
        return jnp.where(column == tens * 16 + (place - tens * 10), 1.0, 0.0).astype(jnp.bfloat16)

    def settle(picker, block):
        return jnp.dot(picker, block, preferred_element_type=jnp.float32).astype(jnp.bfloat16)

    pick80 = ten(80, 128)
    for step in range(1, 8):
        q_arrival(step).wait_recv()
    wq[z] = settle(pick80, q_box[...].reshape(128, 512))

    def ring(buf, ssem, rsem, way, step, arriving):
        gone = step if arriving else step - 1
        src = (z + NZ - gone) % NZ if way == 0 else (z + gone) % NZ
        where = dev(xh, y, up if way == 0 else down, fs)
        return copy(buf.at[src], buf.at[src], ssem.at[way, step - 1], rsem.at[way, step - 1], where)

    wo_mine = wo.at[core]
    streams = ((wq, zq_send, zq_recv), (wo_mine, zo_send, zo_recv), (wm, zm_send, zm_recv))
    for way in range(2):
        ring(*streams[0], way, 1, False).start()

    for c in range(2):
        for k in range(16):
            dx, dl, dy = o_steps[k]
            here = (core + dl) % 2 == xlo
            if dx or dy:
                cond = here
            else:
                cond = here & (core * 2 + c != fs)

            @pl.when(cond)
            def _():
                o_arrival(c, k).wait_recv()
    left = o_box[0].reshape(128, 384)
    right = o_box[1].reshape(128, 384)
    wo[core, z, :, 0:256] = settle(pick80, left[:, 0:256])
    wo[core, z, :, 256:384] = settle(pick80, left[:, 256:384] + right[:, 0:128])
    wo[core, z, :, 384:640] = settle(pick80, right[:, 128:384])
    for way in range(2):
        ring(*streams[1], way, 1, False).start()

    for j in range(4):
        @pl.when((j != fs) | (y != fs))
        def _():
            m_arrival(j).wait_recv()
    wm[z] = settle(ten(40, 64), m_box[...].reshape(64, 1280))
    for way in range(2):
        ring(*streams[2], way, 1, False).start()

    def share(place, slot):
        return copy(
            wo.at[core, place], wo.at[core, place], s_send.at[slot], s_recv.at[slot], dev(xh, y, z, xlo * 2 + 1 - core)
        )

    def shared(place, slot):
        return copy(
            wo.at[1 - core, place], wo.at[1 - core, place], s_send.at[slot], s_recv.at[slot],
            dev(xh, y, z, xlo * 2 + 1 - core),
        )

    share(z, 0).start()
    last = (8, 7)
    for step in range(1, 9):
        for index, stream in enumerate(streams):
            for way in range(2):
                if step <= last[way]:
                    ring(*stream, way, step, True).wait_recv()
                    if step < last[way]:
                        ring(*stream, way, step + 1, False).start()
                    if index == 1:
                        place = (z + NZ - step) % NZ if way == 0 else (z + step) % NZ
                        share(place, step + 8 * way).start()
    for step in range(1, 8):
        for one in n_pair(step, False):
            one.wait_recv()
    shared(z, 0).wait_recv()
    for way in range(2):
        for step in range(1, last[way] + 1):
            place = (z + NZ - step) % NZ if way == 0 else (z + step) % NZ
            shared(place, step + 8 * way).wait_recv()

    for step in range(1, 8):
        q_copy(step).wait_send()
        for one in n_pair(step, True):
            one.wait_send()
    for k in range(16):
        cond = o_remote(k)
        if cond is None:
            o_copy(k).wait_send()
        else:
            @pl.when(cond)
            def _():
                o_copy(k).wait_send()
    for dy in range(1, 4):
        m_copy(dy).wait_send()

    @pl.when(fs != y)
    def _():
        m_copy(0).wait_send()

    share(z, 0).wait_send()
    for way in range(2):
        for step in range(1, last[way] + 1):
            for stream in streams:
                ring(*stream, way, step, False).wait_send()
            place = (z + NZ - step) % NZ if way == 0 else (z + step) % NZ
            share(place, step + 8 * way).wait_send()


def gather_all(q_in, o_in, m_in, normed, seg):
    bf = jnp.bfloat16
    dma = pltpu.SemaphoreType.DMA
    return pl.pallas_call(
        gather_kernel,
        out_shape=[
            jax.ShapeDtypeStruct((NZ, 80, 512), bf),
            jax.ShapeDtypeStruct((2, NZ, 80, 640), bf),
            jax.ShapeDtypeStruct((NZ, 40, 1280), bf),
            jax.ShapeDtypeStruct((8, 128, 1280), bf),
            jax.ShapeDtypeStruct((8, 8, 128), jnp.int32),
        ],
        in_specs=[pl.BlockSpec(memory_space=pltpu.VMEM)] * 5,
        out_specs=[pl.BlockSpec(memory_space=pltpu.VMEM)] * 5,
        scratch_shapes=[
            pltpu.VMEM((8, 16, 512), bf),
            pltpu.VMEM((2, 8, 16, 384), bf),
            pltpu.VMEM((4, 16, 1280), bf),
            dma((8,)), dma((8,)), dma((16,)), dma((2, 16)), dma((4,)), dma((4,)),
            dma((8,)), dma((8,)), dma((8,)), dma((8,)),
            dma((2, 8)), dma((2, 8)), dma((2, 8)), dma((2, 8)), dma((2, 8)), dma((2, 8)),
            dma((17,)), dma((17,)),
        ],
        compiler_params=pltpu.CompilerParams(collective_id=1, has_side_effects=True),
    )(q_in, o_in, m_in, normed, seg)


CH = 5
CW = 256


def deliver_kernel(
    merged_ref, slots_ref, out_ref, rows, keys, picked, landed, zs_send, zs_recv, ks_send, ks_recv, p_send, p_recv
):
    xh, y, z, fs = coords()
    mine = xh * 4 + y
    up = y * NZ + (z + 1) % NZ
    down = y * NZ + (z + NZ - 1) % NZ

    barrier = pltpu.get_barrier_semaphore()
    for peer in (up, down):
        pl.semaphore_signal(barrier, inc=1, device_id=(xh, peer, fs), device_id_type=MESH)
    for step in range(1, 8):
        other = (mine + step) % 8
        pl.semaphore_signal(barrier, inc=1, device_id=(other // 4, other % 4 * NZ + z, fs), device_id_type=MESH)
    for c in range(CH):
        rows[c, pl.ds(pl.multiple_of(z * 32, 32), 32), :] = merged_ref[:, c * CW : (c + 1) * CW]
    keys[z] = slots_ref[...]
    pl.semaphore_wait(barrier, 9)

    def key_copy(way, step):
        src = (z + NZ - (step - 1)) % NZ if way == 0 else (z + step - 1) % NZ
        return pltpu.make_async_remote_copy(
            src_ref=keys.at[src],
            dst_ref=keys.at[src],
            send_sem=ks_send.at[way, step - 1],
            recv_sem=ks_recv.at[way, step - 1],
            device_id=(xh, up if way == 0 else down, fs),
            device_id_type=MESH,
        )

    def row_copy(c, way, step):
        src = (z + NZ - (step - 1)) % NZ if way == 0 else (z + step - 1) % NZ
        piece = rows.at[c, pl.ds(pl.multiple_of(src * 32, 32), 32), :]
        return pltpu.make_async_remote_copy(
            src_ref=piece,
            dst_ref=piece,
            send_sem=zs_send.at[c, way, step - 1],
            recv_sem=zs_recv.at[c, way, step - 1],
            device_id=(xh, up if way == 0 else down, fs),
            device_id_type=MESH,
        )

    def row_arrival(c, way, step):
        src = (z + NZ - step) % NZ if way == 0 else (z + step) % NZ
        piece = rows.at[c, pl.ds(pl.multiple_of(src * 32, 32), 32), :]
        return pltpu.make_async_remote_copy(
            src_ref=piece,
            dst_ref=piece,
            send_sem=zs_send.at[c, way, step - 1],
            recv_sem=zs_recv.at[c, way, step - 1],
            device_id=(xh, up if way == 0 else down, fs),
            device_id_type=MESH,
        )

    def key_arrival(way, step):
        src = (z + NZ - step) % NZ if way == 0 else (z + step) % NZ
        return pltpu.make_async_remote_copy(
            src_ref=keys.at[src],
            dst_ref=keys.at[src],
            send_sem=ks_send.at[way, step - 1],
            recv_sem=ks_recv.at[way, step - 1],
            device_id=(xh, up if way == 0 else down, fs),
            device_id_type=MESH,
        )

    def plane_copy(c, step):
        other = (mine + step) % 8
        return pltpu.make_async_remote_copy(
            src_ref=picked.at[c, pl.ds(pl.multiple_of(other * 32, 32), 32), :],
            dst_ref=landed.at[c, pl.ds(pl.multiple_of(mine * 32, 32), 32), :],
            send_sem=p_send.at[c, step - 1],
            recv_sem=p_recv.at[c, step - 1],
            device_id=(other // 4, other % 4 * NZ + z, fs),
            device_id_type=MESH,
        )

    def plane_arrival(c, step):
        other = (mine + 8 - step) % 8
        return pltpu.make_async_remote_copy(
            src_ref=picked.at[c, pl.ds(pl.multiple_of(other * 32, 32), 32), :],
            dst_ref=landed.at[c, pl.ds(pl.multiple_of(other * 32, 32), 32), :],
            send_sem=p_send.at[c, step - 1],
            recv_sem=p_recv.at[c, step - 1],
            device_id=(other // 4, other % 4 * NZ + z, fs),
            device_id_type=MESH,
        )

    last = (8, 7)
    key_copy(0, 1).start()
    key_copy(1, 1).start()
    for c in range(CH):
        for way in range(2):
            row_copy(c, way, 1).start()
    for step in range(1, 9):
        for way in range(2):
            if step <= last[way]:
                key_arrival(way, step).wait_recv()
                if step < last[way]:
                    key_copy(way, step + 1).start()
        if step == 8:
            pieces = [keys[4 * q, 0:1, :] + keys[4 * q + 1, 0:1, :] + keys[4 * q + 2, 0:1, :] + keys[4 * q + 3, 0:1, :] for q in range(4)]
            row_key = jnp.concatenate(pieces, axis=1)
            place = lax.broadcasted_iota(jnp.int32, (256, 512), 0)
            column = lax.broadcasted_iota(jnp.int32, (256, 512), 1)
            wanted = (place & 224) + 2 * z + (place & 1) + 1
            same = ((place >> 1) & 15) == (column >> 5)
            chosen = jnp.where(same & (row_key == wanted), 1.0, 0.0).astype(jnp.bfloat16)
        for c in range(CH):
            for way in range(2):
                if step <= last[way]:
                    row_arrival(c, way, step).wait_recv()
                    if step < last[way]:
                        row_copy(c, way, step + 1).start()
            if step == 8:
                picked[c] = jnp.dot(chosen, rows[c], preferred_element_type=jnp.float32).astype(jnp.bfloat16)
                for hop in range(1, 8):
                    plane_copy(c, hop).start()
    for c in range(CH):
        own = pl.ds(pl.multiple_of(mine * 32, 32), 32)
        landed[c, own, :] = picked[c, own, :]
        for step in range(1, 8):
            plane_arrival(c, step).wait_recv()
        out_ref[:, c * CW : (c + 1) * CW] = landed[c]
    for way in range(2):
        for step in range(1, last[way] + 1):
            key_copy(way, step).wait_send()
            for c in range(CH):
                row_copy(c, way, step).wait_send()
    for c in range(CH):
        for step in range(1, 8):
            plane_copy(c, step).wait_send()


def deliver(merged, slots):
    width = merged.shape[1]
    return pl.pallas_call(
        deliver_kernel,
        out_shape=jax.ShapeDtypeStruct((256, width), jnp.bfloat16),
        in_specs=[pl.BlockSpec(memory_space=pltpu.VMEM)] * 2,
        out_specs=pl.BlockSpec(memory_space=pltpu.VMEM),
        scratch_shapes=[
            pltpu.VMEM((CH, 512, CW), jnp.bfloat16),
            pltpu.VMEM((NZ, 8, 128), jnp.int32),
            pltpu.VMEM((CH, 256, CW), jnp.bfloat16),
            pltpu.VMEM((CH, 256, CW), jnp.bfloat16),
            pltpu.SemaphoreType.DMA((CH, 2, 8)),
            pltpu.SemaphoreType.DMA((CH, 2, 8)),
            pltpu.SemaphoreType.DMA((2, 8)),
            pltpu.SemaphoreType.DMA((2, 8)),
            pltpu.SemaphoreType.DMA((CH, 7)),
            pltpu.SemaphoreType.DMA((CH, 7)),
        ],
        compiler_params=pltpu.CompilerParams(collective_id=0, has_side_effects=True),
    )(merged, slots)


def normalize(values_in, gain_row):
    widened = values_in.astype(jnp.float32)
    centered = widened - jnp.mean(widened, axis=1, keepdims=True)
    variance = jnp.mean(centered * centered, axis=1, keepdims=True)
    return (centered * lax.rsqrt(variance + epsilon) * gain_row).astype(jnp.bfloat16)


def attend(queries, keys_all, values_all, segs):
    factor = 1.0 / math.sqrt(HD)
    allowed = segs[:, None] == segs[None, :]
    pieces = []
    for head_index in range(queries.shape[1] // HD):
        first_col = head_index * HD
        last_col = first_col + HD
        scores = (
            lax.dot_general(
                queries[:, first_col:last_col],
                keys_all[:, first_col:last_col],
                (((1,), (1,)), ((), ())),
                preferred_element_type=jnp.float32,
            )
            * factor
        )
        masked = jnp.where(allowed, scores, -jnp.inf)
        highest = jnp.max(masked, axis=1, keepdims=True)
        weights = jnp.exp(masked - highest)
        totals = jnp.sum(weights, axis=1, keepdims=True)
        head_out = jnp.dot(
            weights.astype(jnp.bfloat16),
            values_all[:, first_col:last_col],
            preferred_element_type=jnp.float32,
        )
        pieces.append(head_out / totals)
    return jnp.concatenate(pieces, axis=1).astype(jnp.bfloat16)


def mix(left, right):
    return jnp.dot(left, right, preferred_element_type=jnp.float32)


def per_device(
    tokens, qkv_weight, out_weight, merge_weight, ln_gains, segments, merge_rows, owners
):
    bf = jnp.bfloat16
    xh = lax.axis_index("xh")
    fs = lax.axis_index("fsdp")
    z = lax.axis_index("yz") % NZ
    place = jnp.arange(1280, dtype=jnp.int32)
    natural = ((place % 80 // 10) * NZ + place // 80) * 10 + place % 10
    unmove = (natural[:, None] == jnp.arange(1280, dtype=jnp.int32)[None, :]).astype(bf)
    move = (natural[None, :] == jnp.arange(1280, dtype=jnp.int32)[:, None]).astype(bf)

    q_in = qkv_weight.reshape(3, 10, 2, 160).transpose(2, 1, 0, 3).reshape(2, 10, 480)
    q_in = jnp.pad(q_in, ((0, 0), (0, 6), (0, 32)))
    o_flat = out_weight.T
    o_in = jnp.where(fs % 2 == 0, jnp.pad(o_flat, ((0, 6), (0, 64))), jnp.pad(o_flat, ((0, 6), (64, 0))))
    m_in = jnp.pad(merge_weight, ((0, 6), (0, 0)))
    normed = mix(normalize(tokens, ln_gains[0]), move).astype(bf)
    tokens_moved = mix(tokens, move)
    gains_moved = jnp.sum(jnp.where(natural[:, None] == jnp.arange(1280)[None, :], ln_gains[1][None, :], 0.0), axis=1)
    seg_in = jnp.broadcast_to(segments, (8, 128))
    wq, wo, wm, normed_all, seg_all = gather_all(q_in, o_in, m_in, normed, seg_in)
    wq = wq.reshape(1280, 512)
    group_segs = seg_all[:, 0, :].reshape(2, 512)
    qkv = mix(normed_all.reshape(1024, 1280), wq).astype(bf)
    attended = []
    for g in range(2):
        mine = qkv[g * 512 : (g + 1) * 512]
        attended.append(attend(mine[:, 0:160], mine[:, 160:320], mine[:, 320:480], group_segs[g]))
    attended = jnp.concatenate(attended, axis=0).reshape(8, 128, 160)
    received = lax.all_to_all(attended, XG, split_axis=0, concat_axis=0, tiled=True)
    local = received.reshape(2, 4, 128, 160).transpose(2, 1, 0, 3).reshape(128, 1280)
    wo = wo.reshape(2, 1280, 640)
    update = lax.dot_general(local[:, :640], wo[0], (((1,), (1,)), ((), ())), preferred_element_type=jnp.float32)
    update = update + lax.dot_general(local[:, 640:], wo[1], (((1,), (1,)), ((), ())), preferred_element_type=jnp.float32)
    layer_out = (tokens_moved + update).astype(bf)
    merge_in = normalize(layer_out, gains_moved)
    order = merge_rows[0].reshape(32, 4).T.reshape(128)
    picker = (order[:, None] == jnp.arange(128, dtype=jnp.int32)[None, :]).astype(bf)
    stacked = mix(mix(picker, merge_in).astype(bf), unmove).astype(bf)
    blocks = stacked.reshape(4, 32, 2, 640).transpose(0, 2, 1, 3).reshape(8, 32, 640)
    inputs = lax.all_to_all(blocks, XG, split_axis=0, concat_axis=0, tiled=True).reshape(256, 640)
    partial = mix(inputs, wm.reshape(640, 1280)).astype(bf).reshape(8, 32, 1280)
    parts = lax.all_to_all(partial, XG, split_axis=0, concat_axis=0, tiled=True)
    merged = jnp.sum(parts.astype(jnp.float32), axis=0).astype(bf)
    targets = owners[:, 0]
    ranks = jnp.arange(32)
    position = jnp.sum((targets[:, None] == targets[None, :]) & (ranks[None, :] < ranks[:, None]), axis=1)
    slot_row = targets * 2 + position.astype(jnp.int32) + 1
    spread = jnp.where(jnp.arange(4)[:, None] == z % 4, slot_row[None, :], 0).reshape(1, 128)
    return deliver(merged, jnp.broadcast_to(spread, (8, 128)))


def solution(mesh):
    cut = Mesh(mesh.devices.reshape(2, 64, 4), ("xh", "yz", "fsdp"))
    every = ("xh", "yz", "fsdp")
    return jax.shard_map(
        per_device,
        mesh=cut,
        in_specs=(
            P(every, None),
            P(None, ("xh", "yz"), "fsdp"),
            P("fsdp", ("xh", "yz")),
            P(every, None),
            P(),
            P(("xh", "yz"), "fsdp"),
            P(every, None),
            P(every, None),
        ),
        out_specs=P(every, None),
        check_vma=False,
    )
```

time: 751 us -> 188 us (0.25)
  blocking collectives: 329 us -> 0 us
  waiting for transfers between devices: 283 us -> 20.9 us
  Pallas kernels: 57.1 us -> 118 us
  local copies, waits for them, and re-layouts: 40.8 us -> 12.7 us
  between operations: 13.5 us -> 0.23 us
    all_gather x2 -> x0, blocking collectives: 329 us -> none  [the longest x1 324 us: per_device(): out_mine = lax.all_gather(out_weight, 'dp', axis=1, tiled=True)]
    all_gather x4 -> x0, waiting for transfers between devices: 256 us -> none  [the longest x1 217 us: per_device(): part_rows = lax.all_gather(merge_weight, 'dp', axis=0, tiled=True)]
    pallas_call x0 -> x1, Pallas kernels: none -> 76.9 us  [gather_all(): pl.pallas_call(gather_kernel, out_shape=[jax.ShapeDtypeStruct((NZ, 80, 51...]
    unnamed x20 -> x14, local copies, waits for them, and re-layouts: 22.2 us -> 2.53 us
    reduce_scatter x1 -> x0, waiting for transfers between devices: 19.3 us -> none  [per_device(): lax.psum_scatter(jnp.dot(gathered_inputs, part_rows, preferred_element_ty...]
    pallas_call x1, Pallas kernels: 57.1 us -> 41 us  [deliver(): pl.pallas_call(deliver_kernel, out_shape=jax.ShapeDtypeStruct((256, width...]
    all_to_all x2 -> x3, waiting for transfers between devices: 6.51 us -> 20.9 us  [the longest x1 11.3 us: per_device(): parts = lax.all_to_all(partial, XG, split_axis=0, concat_axis=0, tiled=True)]
  transfers between devices with their start and end apart: 7 -> 3, of which waited for: 4 -> 3; matrix products, arithmetic and copies ran while one was open for 7% -> 4% of each run, Pallas kernels for 0% -> 0%
where the time goes in v2:
time: 188 us; the launch traced here: 187 us
  Pallas kernels  118 us (63%)
  waiting for transfers between devices  20.9 us (11%)
  matrix products  15.8 us (8%)
  local copies, waits for them, and re-layouts  12.7 us (7%)
  starting transfers between devices  11.2 us (6%)
  other arithmetic  8.19 us (4%)
    pallas_call x1, Pallas kernels, gather_all(): pl.pallas_call(gather_kernel, out_shape=[jax.ShapeDtypeStruct((NZ, 80, 51...  76.9 us
    pallas_call x1, Pallas kernels, deliver(): pl.pallas_call(deliver_kernel, out_shape=jax.ShapeDtypeStruct((256, width...  41 us
    dot_general x5, matrix products, mix(): return jnp.dot(left, right, preferred_element_type=jnp.float32)  11.9 us
    all_to_all x1, waiting for transfers between devices, per_device(): parts = lax.all_to_all(partial, XG, split_axis=0, concat_axis=0, tiled=True)  11.3 us
    all_to_all x1, waiting for transfers between devices, per_device(): lax.all_to_all(blocks, XG, split_axis=0, concat_axis=0, tiled=True)  8.13 us
    all_to_all x1, starting transfers between devices, per_device(): lax.all_to_all(attended, XG, split_axis=0, concat_axis=0, tiled=True)  4.26 us
  transfers between devices with their start and end apart: 3, of which 3 were waited for; matrix products, arithmetic and copies ran while one was open for 4% of the time, Pallas kernels for 0%

profile of v2, /device:TPU:24, one launch (start us, length us, event | category | flops | bytes accessed | tf_op | source)
XLA Modules:
  0.0 187.0 jit_solution(11826242883573673496)
XLA Ops:
  0.0 0.8 slice_reduce_fusion
  0.8 1.1 convert_reduce_fusion
  2.0 1.2 fusion.34
  3.2 0.9 reshape.186
  4.2 0.6 pad.16.q_in
  4.8 1.4 pad.19.m_in
  6.2 1.5 pad_select_fusion.o_in
  7.6 3.2 %fusion.14.normed_in = bf16[128,1280]{1,0:T(8,128)(2,1)} fusion(s32[1280]{0:T(1024)S(1)} %fusion.85, bf16[128,1280]{1,0:T(8,128)(2,1)} %param.8, f32[1280]{0:T(1024)S(1)} %get-tuple-element.16, f32[128]{0:T(128)S(1)} %add_rsqrt_fusion.1, f32[128]{0:T(128)S(1)} %broadcast_multiply_fusion.1), kind=kOutput, calls=%fused_computation.16 | convolution fusion | flops 422051840 | bytes 666624 | tf_op jit(solution)/shard_map/dot_general | solution.py:478
  10.9 0.6 broadcast_in_dim.41.seg_in
  11.5 76.9 %shard_map.82 = (bf16[16,80,512]{2,1,0:T(8,128)(2,1)}, bf16[2,16,80,640]{3,2,1,0:T(8,128)(2,1)}, bf16[16,40,1280]{2,1,0:T(8,128)(2,1)}, bf16[8,128,1280]{2,1,0:T(8,128)(2,1)}, s32[8,8,128]{2,1,0:T(8,128)}) custom-call(bf16[2,16,512]{2,1,0:T(8,128)(2,1)} %pad.16.q_in, bf16[16,384]{1,0:T(8,128)(2,1)} %pad_select_fusion.o_in, bf16[16,1280]{1,0:T(8,128)(2,1)} %pad.19.m_in, ...), custom_call_target="tpu_custom_call" | custom-call | tf_op jit(solution)/shard_map/pallas_call | solution.py:257
  88.4 0.7 fusion.96
  89.2 3.7 %convolution_convert_fusion.2 = bf16[1024,512]{0,1:T(8,128)(2,1)S(1)} fusion(bf16[1024,1280]{1,0:T(8,128)(2,1)} %bitcast.52, bf16[1280,512]{1,0:T(8,128)(2,1)} %bitcast.53), kind=kOutput, calls=%fused_computation.19 | convolution fusion | flops 1342701568 | bytes 4980736 | tf_op jit(solution)/shard_map/dot_general | solution.py:478
  96.3 0.8 copy_bitcast_fusion
  97.1 4.3 %all-to-all-start = ((bf16[8,128,160]{1,2,0:T(8,128)(2,1)}), bf16[8,128,160]{1,2,0:T(8,128)(2,1)}, u32[]{:S(2)}, u32[]{:S(2)}) async-start(bf16[8,128,160]{1,2,0:T(8,128)(2,1)} %copy_bitcast_fusion), calls=%async_computation | async-start | bytes 655360 | tf_op jit(solution)/shard_map/all_to_all | solution.py:511
  101.4 2.3 %fusion.95 = (bf16[1,16,80,640]{3,2,1,0:T(8,128)(2,1)S(1)}, bf16[1,16,80,640]{3,2,1,0:T(8,128)(2,1)S(1)}) fusion(bf16[2,16,80,640]{3,2,1,0:T(8,128)(2,1)} %get-tuple-element.13), kind=kLoop, calls=%fused_computation.127 | loop fusion | bytes 6553600 | tf_op jit(solution)/shard_map/slice | solution.py:515
  103.7 1.9 %fusion.9 = f32[128,1280]{0,1:T(8,128)} fusion(bf16[128,1280]{1,0:T(8,128)(2,1)S(1)} %copy-done.1, s32[1280]{0:T(1024)S(1)} %fusion.85), kind=kOutput, calls=%fused_computation.13 | convolution fusion | flops 422707200 | bytes 988160 | tf_op jit(solution)/shard_map/dot_general | solution.py:478
  106.1 0.6 reduce.8
  107.0 1.0 select_reduce_fusion
  108.0 1.4 all-to-all-done
  109.4 1.1 copy.31
  110.5 0.6 fusion.56
  111.1 0.6 fusion.101
  111.9 1.6 fusion.15
  113.6 0.8 copy.34
  114.3 3.4 %all-to-all-start.1 = ((bf16[8,32,640]{2,1,0:T(8,128)(2,1)}), bf16[8,32,640]{2,1,0:T(8,128)(2,1)S(1)}, u32[]{:S(2)}, u32[]{:S(2)}) async-start(bf16[8,32,640]{2,1,0:T(8,128)(2,1)} %bitcast.15), calls=%async_computation.1 | async-start | bytes 655360 | tf_op jit(solution)/shard_map/all_to_all | solution.py:522
  117.8 8.1 %all-to-all-done.1 = bf16[8,32,640]{2,1,0:T(8,128)(2,1)S(1)} async-done(((bf16[8,32,640]{2,1,0:T(8,128)(2,1)}), bf16[8,32,640]{2,1,0:T(8,128)(2,1)S(1)}, u32[]{:S(2)}, u32[]{:S(2)}) %all-to-all-start.1) | async-done | bytes 327712 | tf_op jit(solution)/shard_map/all_to_all | solution.py:522
  125.9 1.5 convolution_convert_fusion
  127.5 3.5 %all-to-all-start.2 = ((bf16[8,32,1280]{2,1,0:T(8,128)(2,1)}), bf16[8,32,1280]{2,1,0:T(8,128)(2,1)S(1)}, u32[]{:S(2)}, u32[]{:S(2)}) async-start(bf16[8,32,1280]{2,1,0:T(8,128)(2,1)} %bitcast.18), calls=%async_computation.2 | async-start | bytes 1310720 | tf_op jit(solution)/shard_map/all_to_all | solution.py:524
  131.4 11.3 %all-to-all-done.2 = bf16[8,32,1280]{2,1,0:T(8,128)(2,1)S(1)} async-done(((bf16[8,32,1280]{2,1,0:T(8,128)(2,1)}), bf16[8,32,1280]{2,1,0:T(8,128)(2,1)S(1)}, u32[]{:S(2)}, u32[]{:S(2)}) %all-to-all-start.2) | async-done | bytes 655392 | tf_op jit(solution)/shard_map/all_to_all | solution.py:524
  142.7 0.7 reduce_sum.111.merged_ref
  144.0 41.0 %shard_map.83 = bf16[256,1280]{1,0:T(8,128)(2,1)} custom-call(bf16[32,1280]{1,0:T(8,128)(2,1)} %reduce_sum.111.merged_ref, s32[8,128]{1,0:T(8,128)} %broadcast_in_dim.86.slots_ref), custom_call_target="tpu_custom_call" | custom-call | tf_op jit(solution)/shard_map/pallas_call | solution.py:420
  185.0 2.0 %copy.42 = bf16[256,1280]{1,0:T(8,128)(2,1)} copy(bf16[256,1280]{1,0:T(8,128)(2,1)} %shard_map.83) | data formatting | bytes 1310720
  (43 shorter events, 5.7 us)
Async XLA Ops:
  7.6 3.3 %copy-start.3 = (s32[1,128]{1,0:T(1,128)S(1)}, s32[1,128]{1,0:T(1,128)}, u32[]{:S(2)}) copy-start(s32[1,128]{1,0:T(1,128)} %param.13) | copy-start | bytes 1540
  97.1 12.3 %all-to-all-start = ((bf16[8,128,160]{1,2,0:T(8,128)(2,1)}), bf16[8,128,160]{1,2,0:T(8,128)(2,1)}, u32[]{:S(2)}, u32[]{:S(2)}) async-start(bf16[8,128,160]{1,2,0:T(8,128)(2,1)} %copy_bitcast_fusion), calls=%async_computation | async-start | bytes 655360 | tf_op jit(solution)/shard_map/all_to_all | solution.py:511
  101.4 2.3 %copy-start.1 = (bf16[128,1280]{1,0:T(8,128)(2,1)S(1)}, bf16[128,1280]{1,0:T(8,128)(2,1)}, u32[]{:S(2)}) copy-start(bf16[128,1280]{1,0:T(8,128)(2,1)} %param.8) | copy-start | bytes 983044
  103.7 2.4 %copy-start.4 = (s32[1,128]{1,0:T(1,128)S(1)}, s32[1,128]{1,0:T(1,128)}, u32[]{:S(2)}) copy-start(s32[1,128]{1,0:T(1,128)} %param.14) | copy-start | bytes 1540
  109.4 1.7 copy-start.2
  113.5 12.5 %copy-start = (bf16[16,40,1280]{2,1,0:T(8,128)(2,1)S(1)}, bf16[16,40,1280]{2,1,0:T(8,128)(2,1)}, u32[]{:S(2)}) copy-start(bf16[16,40,1280]{2,1,0:T(8,128)(2,1)} %get-tuple-element.14) | copy-start | bytes 4915204
  114.3 11.6 %all-to-all-start.1 = ((bf16[8,32,640]{2,1,0:T(8,128)(2,1)}), bf16[8,32,640]{2,1,0:T(8,128)(2,1)S(1)}, u32[]{:S(2)}, u32[]{:S(2)}) async-start(bf16[8,32,640]{2,1,0:T(8,128)(2,1)} %bitcast.15), calls=%async_computation.1 | async-start | bytes 655360 | tf_op jit(solution)/shard_map/all_to_all | solution.py:522
  125.9 5.1 %copy-start.5 = (s32[32,1]{0,1:T(1,128)S(1)}, s32[32,1]{0,1:T(1,128)}, u32[]{:S(2)}) copy-start(s32[32,1]{0,1:T(1,128)} %param.15) | copy-start | bytes 388
  127.5 15.2 %all-to-all-start.2 = ((bf16[8,32,1280]{2,1,0:T(8,128)(2,1)}), bf16[8,32,1280]{2,1,0:T(8,128)(2,1)S(1)}, u32[]{:S(2)}, u32[]{:S(2)}) async-start(bf16[8,32,1280]{2,1,0:T(8,128)(2,1)} %bitcast.18), calls=%async_computation.2 | async-start | bytes 1310720 | tf_op jit(solution)/shard_map/all_to_all | solution.py:524

commit v3 on v0

v3 whole, which is shorter than its diff:
```python
import math

import jax
import jax.numpy as jnp
from jax import lax
from jax.experimental import pallas as pl
from jax.experimental.pallas import tpu as pltpu
from jax.sharding import Mesh
from jax.sharding import PartitionSpec as P

HD = 80
NZ = 16
NY = 4
CH = 5
CW = 256
MESH = pl.DeviceIdType.MESH
epsilon = 1e-06


def coords():
    yz = lax.axis_index("yz")
    return lax.axis_index("xh"), yz // NZ, yz % NZ, lax.axis_index("fsdp")


def rows_of(place, n):
    return pl.ds(pl.multiple_of(place * n, n), n)


def center(values):
    middle = values - jnp.mean(values, axis=1, keepdims=True)
    variance = jnp.mean(middle * middle, axis=1, keepdims=True)
    return middle * lax.rsqrt(variance + epsilon)


def mix(left, right):
    return jnp.dot(left, right, preferred_element_type=jnp.float32)


def mix_t(left, right):
    return lax.dot_general(left, right, (((1,), (1,)), ((), ())), preferred_element_type=jnp.float32)


def block_kernel(
    tok_in, gain_in, q_in, o_in, m_in, seg_in, order_in, slot_in, out,
    wq, wo, wm, unmove, tok_t, normed_all, seg_all, q_box, o_box, m_box, slots,
    qkv, att_out, att_in, mi_out, mi_in, part_out, part_in, rows, picked, landed,
    q_send, q_recv, o_send, o_recv, m_send, m_recv, n_send, n_recv, g_send, g_recv,
    zq_send, zq_recv, zo_send, zo_recv, zm_send, zm_recv, s_send, s_recv,
    k_send, k_recv, a_send, a_recv, i_send, i_recv, r_send, r_recv, p_send, p_recv, z_send, z_recv,
):
    bf = jnp.bfloat16
    xh, y, z, fs = coords()
    core = fs % 2
    xlo = fs // 2
    mine = xh * 4 + y
    member = xh * 4 + fs
    up, down = (z + 1) % NZ, (z + NZ - 1) % NZ

    def dev(xh_, y_, z_, fs_):
        return (xh_, y_ * NZ + z_, fs_)

    barrier = pltpu.get_barrier_semaphore()
    for dx in range(2):
        for dy in range(4):
            for df in range(4):
                if dx or dy or df:
                    there = dev((xh + dx) % 2, (y + dy) % 4, z, (fs + df) % 4)
                    pl.semaphore_signal(barrier, inc=1, device_id=there, device_id_type=MESH)
    for dz in range(1, NZ):
        pl.semaphore_signal(barrier, inc=1, device_id=dev(xh, y, (z + dz) % NZ, fs), device_id_type=MESH)

    lane = lax.broadcasted_iota(jnp.int32, (128, 128), 1)
    for b in range(10):
        p = lax.broadcasted_iota(jnp.int32, (128, 128), 0) + b * 128
        pz = ((p >> 4) * 52429) >> 18
        rest = p - pz * 80
        tens = (rest * 52429) >> 19
        natural = (tens * NZ + pz) * 10 + (rest - tens * 10)
        for t in range(10):
            unmove[b * 128 : (b + 1) * 128, t * 128 : (t + 1) * 128] = jnp.where(
                natural == lane + t * 128, 1.0, 0.0
            ).astype(bf)
    normed = (center(tok_in[...].astype(jnp.float32)) * gain_in[0:1, :]).astype(bf)
    normed_all[member] = mix_t(normed, unmove[...]).astype(bf)
    seg_all[member] = seg_in[...]
    slots[mine] = slot_in[...]
    pl.semaphore_wait(barrier, 46)

    def copy(src, dst, ssem, rsem, where):
        return pltpu.make_async_remote_copy(
            src_ref=src, dst_ref=dst, send_sem=ssem, recv_sem=rsem, device_id=where, device_id_type=MESH
        )

    def q_copy(step):
        dx, dy = step // 4, step % 4
        oxh, oy = (xh + dx) % 2, (y + dy) % 4
        return copy(q_in.at[oxh], q_box.at[mine], q_send.at[step], q_recv.at[step], dev(oxh, oy, z, fs))

    def q_arrival(step):
        dx, dy = step // 4, step % 4
        oxh, oy = (xh + dx) % 2, (y + 4 - dy) % 4
        return copy(q_in.at[xh], q_box.at[oxh * 4 + oy], q_send.at[step], q_recv.at[step], dev(oxh, oy, z, fs))

    for step in range(1, 8):
        q_copy(step).start()
    q_box[mine] = q_in[xh]

    o_steps = [(dx, dl, dy) for dx in range(2) for dl in range(2) for dy in range(4)]

    def o_slot(c, d):
        return o_box.at[c, d]

    def o_copy(k):
        dx, dl, dy = o_steps[k]
        oxh, olo, oy = (xh + dx) % 2, (xlo + dl) % 2, (y + dy) % 4
        return copy(o_in, o_slot(core, mine), o_send.at[k], o_recv.at[core, k], dev(oxh, oy, z, olo * 2 + xlo))

    def o_arrival(c, k):
        dx, dl, dy = o_steps[k]
        oxh, oy = (xh + dx) % 2, (y + 4 - dy) % 4
        return copy(o_in, o_slot(c, oxh * 4 + oy), o_send.at[k], o_recv.at[c, k], dev(oxh, oy, z, core * 2 + c))

    def o_remote(k):
        dx, dl, dy = o_steps[k]
        if dx or dy:
            return None
        return (xlo + dl) % 2 * 2 + xlo != fs

    for k in range(16):
        cond = o_remote(k)
        if cond is None:
            o_copy(k).start()
        else:
            @pl.when(cond)
            def _():
                o_copy(k).start()

    @pl.when(xlo == core)
    def _():
        o_box[core, mine] = o_in[...]

    def m_copy(dy):
        return copy(m_in, m_box.at[fs], m_send.at[dy], m_recv.at[fs], dev(xh, (y + dy) % 4, z, y))

    def m_arrival(j):
        return copy(m_in, m_box.at[j], m_send.at[0], m_recv.at[j], dev(xh, fs, z, j))

    for dy in range(1, 4):
        m_copy(dy).start()

    @pl.when(fs != y)
    def _():
        m_copy(0).start()

    @pl.when(fs == y)
    def _():
        m_box[fs] = m_in[...]


    def k_pair(step, to):
        dx, dy = step // 4, step % 4
        oxh = (xh + dx) % 2
        oy = (y + dy) % 4 if to else (y + 4 - dy) % 4
        slot = mine if to else oxh * 4 + oy
        return copy(slot_in, slots.at[slot], k_send.at[step], k_recv.at[step], dev(oxh, oy, z, fs))

    def n_pair(step, to):
        dx, df = step // 4, step % 4
        oxh = (xh + dx) % 2
        ofs = (fs + df) % 4 if to else (fs + 4 - df) % 4
        slot = member if to else oxh * 4 + ofs
        there = dev(oxh, y, z, ofs)
        return (
            copy(normed_all.at[member], normed_all.at[slot], n_send.at[step], n_recv.at[step], there),
            copy(seg_in, seg_all.at[slot], g_send.at[step], g_recv.at[step], there),
        )

    for step in range(1, 8):
        for one in n_pair(step, True):
            one.start()
    for step in range(1, 8):
        k_pair(step, True).start()

    def ten(count, depth):
        place = lax.broadcasted_iota(jnp.int32, (count, depth), 0)
        column = lax.broadcasted_iota(jnp.int32, (count, depth), 1)
        tens = (place * 52429) >> 19
        return jnp.where(column == tens * 16 + (place - tens * 10), 1.0, 0.0).astype(bf)

    def settle(picker, block):
        return mix(picker, block).astype(bf)

    pick80 = ten(80, 128)
    for step in range(1, 8):
        q_arrival(step).wait_recv()
    wq[z] = settle(pick80, q_box[...].reshape(128, 512))

    last = (8, 7)

    def ring(buf, ssem, rsem, way, step, arriving):
        gone = step if arriving else step - 1
        src = (z + NZ - gone) % NZ if way == 0 else (z + gone) % NZ
        where = dev(xh, y, up if way == 0 else down, fs)
        return copy(buf.at[src], buf.at[src], ssem.at[way, step - 1], rsem.at[way, step - 1], where)

    q_ring = (wq, zq_send, zq_recv)
    o_ring = (wo.at[core], zo_send, zo_recv)
    m_ring = (wm, zm_send, zm_recv)
    sibling = dev(xh, y, z, xlo * 2 + 1 - core)

    def share(half, place, slot):
        return copy(wo.at[half, place], wo.at[half, place], s_send.at[slot], s_recv.at[slot], sibling)

    def begin(stream):
        for way in range(2):
            ring(*stream, way, 1, False).start()

    def serve(stream, step):
        for way in range(2):
            if step <= last[way]:
                ring(*stream, way, step, True).wait_recv()
                if step < last[way]:
                    ring(*stream, way, step + 1, False).start()
                if stream is o_ring:
                    place = (z + NZ - step) % NZ if way == 0 else (z + step) % NZ
                    share(core, place, step + 8 * way).start()

    begin(q_ring)
    for c in range(2):
        for k in range(16):
            dx, dl, dy = o_steps[k]
            here = (core + dl) % 2 == xlo
            cond = here if dx or dy else here & (core * 2 + c != fs)

            @pl.when(cond)
            def _():
                o_arrival(c, k).wait_recv()
    left = o_box[0].reshape(128, 384)
    right = o_box[1].reshape(128, 384)
    wo[core, z, :, 0:256] = settle(pick80, left[:, 0:256])
    wo[core, z, :, 256:384] = settle(pick80, left[:, 256:384] + right[:, 0:128])
    wo[core, z, :, 384:640] = settle(pick80, right[:, 128:384])
    begin(o_ring)
    share(core, z, 0).start()
    for j in range(4):
        @pl.when((j != fs) | (y != fs))
        def _():
            m_arrival(j).wait_recv()
    wm[z] = settle(ten(40, 64), m_box[...].reshape(64, 1280))
    tok_t[...] = mix_t(unmove[...], tok_in[...]).astype(bf)

    for step in range(1, 9):
        serve(q_ring, step)
        if step % 2 == 0:
            serve(o_ring, step // 2)
        if step == 6:
            begin(m_ring)
    for step in range(1, 8):
        for one in n_pair(step, False):
            one.wait_recv()

    factor = 1.0 / math.sqrt(HD)

    def a_copy(step, to):
        dx, df = step // 4, step % 4
        oxh = (xh + dx) % 2
        ofs = (fs + df) % 4 if to else (fs + 4 - df) % 4
        head = fs * 2 + xh if to else ofs * 2 + oxh
        return copy(
            att_out.at[oxh * 4 + ofs], att_in.at[rows_of(head, 160), :], a_send.at[step], a_recv.at[step], dev(oxh, y, z, ofs)
        )

    def project(g):
        block = normed_all[g * 4 : (g + 1) * 4].reshape(512, 1280)
        qkv[g] = mix(block, wq[...].reshape(1280, 512)).astype(bf)

    def attend(g):
        across = jnp.concatenate([seg_all[g * 4 + b, 0:1, :] for b in range(4)], axis=1)
        downs = []
        for b in range(4):
            one = jnp.broadcast_to(seg_all[g * 4 + b, 0:1, :].astype(jnp.float32), (128, 128)).T
            downs.append(jnp.concatenate([one] * 4, axis=1))
        allowed = jnp.concatenate(downs, axis=0) == across.astype(jnp.float32)
        for h in range(2):
            query = qkv[g, :, h * HD : h * HD + HD]
            key = qkv[g, :, 160 + h * HD : 160 + h * HD + HD]
            value = qkv[g, :, 320 + h * HD : 320 + h * HD + HD]
            scores = jnp.where(allowed, mix_t(key, query) * factor, -jnp.inf)
            weights = jnp.exp(scores - jnp.max(scores, axis=0, keepdims=True))
            totals = jnp.sum(weights, axis=0, keepdims=True)
            value_t = value.astype(jnp.float32).T.astype(bf)
            head_out = (mix(value_t, weights.astype(bf)) / totals).astype(bf)
            for b in range(4):
                att_out[g * 4 + b, h * HD : h * HD + HD, :] = head_out[:, b * 128 : (b + 1) * 128]

    project(0)
    serve(o_ring, 5)
    attend(0)
    serve(m_ring, 1)
    project(1)
    serve(o_ring, 6)
    attend(1)
    att_in[rows_of(fs * 2 + xh, 160), :] = att_out[member]
    for step in range(1, 8):
        a_copy(step, True).start()
    serve(m_ring, 2)
    serve(o_ring, 7)
    serve(m_ring, 3)
    serve(o_ring, 8)
    for step in range(1, 8):
        a_copy(step, False).wait_recv()
    share(1 - core, z, 0).wait_recv()
    for way in range(2):
        for step in range(1, last[way] + 1):
            place = (z + NZ - step) % NZ if way == 0 else (z + step) % NZ
            share(1 - core, place, step + 8 * way).wait_recv()

    update = mix(wo[0].reshape(1280, 640), att_in[0:640, :]) + mix(wo[1].reshape(1280, 640), att_in[640:1280, :])
    layer_t = (tok_t[...].astype(jnp.float32) + update).astype(bf)
    picker = jnp.where(order_in[...] == lane, 1.0, 0.0).astype(bf)
    chosen = mix_t(picker, layer_t).astype(bf)
    merge_in = (center(mix(chosen, unmove[...])) * gain_in[1:2, :]).astype(bf)
    for b in range(8):
        mi_out[b] = merge_in[b // 2 * 32 : b // 2 * 32 + 32, b % 2 * 640 : b % 2 * 640 + 640]

    def i_copy(step, to):
        dx, df = step // 4, step % 4
        oxh = (xh + dx) % 2
        ofs = (fs + df) % 4 if to else (fs + 4 - df) % 4
        other = oxh * 4 + ofs
        slot = member if to else other
        return copy(mi_out.at[other], mi_in.at[slot], i_send.at[step], i_recv.at[step], dev(oxh, y, z, ofs))

    for step in range(1, 8):
        i_copy(step, True).start()
    mi_in[member] = mi_out[member]
    for step in range(4, 9):
        serve(m_ring, step)
    for step in range(1, 8):
        i_copy(step, False).wait_recv()

    def r_copy(c, step, to):
        dx, df = step // 4, step % 4
        oxh = (xh + dx) % 2
        ofs = (fs + df) % 4 if to else (fs + 4 - df) % 4
        other = oxh * 4 + ofs
        slot = member if to else other
        return copy(
            part_out.at[c, other], part_in.at[c, slot], r_send.at[c, step], r_recv.at[c, step], dev(oxh, y, z, ofs)
        )

    inputs = mi_in[...].reshape(256, 640)
    for c in range(CH):
        part = mix(inputs, wm[:, :, c * CW : (c + 1) * CW].reshape(640, CW)).astype(bf)
        part_out[c] = part.reshape(8, 32, CW)
        for step in range(1, 8):
            r_copy(c, step, True).start()
        part_in[c, member] = part_out[c, member]

    def p_copy(c, step, to):
        dx, dy = step // 4, step % 4
        oxh = (xh + dx) % 2
        oy = (y + dy) % 4 if to else (y + 4 - dy) % 4
        slot = mine if to else oxh * 4 + oy
        return copy(
            rows.at[c, mine], rows.at[c, slot], p_send.at[c, step], p_recv.at[c, step], dev(oxh, oy, z, fs)
        )

    for c in range(CH):
        for step in range(1, 8):
            r_copy(c, step, False).wait_recv()
        rows[c, mine] = jnp.sum(part_in[c].astype(jnp.float32), axis=0).astype(bf)
        for step in range(1, 8):
            p_copy(c, step, True).start()

    def z_copy(c, step, to):
        other = (z + step) % NZ if to else (z + NZ - step) % NZ
        slot = z if to else other
        return copy(
            picked.at[c, rows_of(other, 16), :], landed.at[c, rows_of(slot, 16), :],
            z_send.at[c, step], z_recv.at[c, step], dev(xh, y, other, fs),
        )

    for step in range(1, 8):
        k_pair(step, False).wait_recv()
    row_key = jnp.concatenate(
        [slots[4 * q, 0:1, :] + slots[4 * q + 1, 0:1, :] + slots[4 * q + 2, 0:1, :] + slots[4 * q + 3, 0:1, :] for q in range(2)],
        axis=1,
    )
    place = lax.broadcasted_iota(jnp.int32, (256, 256), 0)
    column = lax.broadcasted_iota(jnp.int32, (256, 256), 1)
    wanted = (mine * NZ + (place >> 4)) * 2 + (place & 1) + 1
    select = jnp.where((((place >> 1) & 7) == (column >> 5)) & (row_key == wanted), 1.0, 0.0).astype(bf)
    for c in range(CH):
        for step in range(1, 8):
            p_copy(c, step, False).wait_recv()
        picked[c] = mix(select, rows[c].reshape(256, CW)).astype(bf)
        for step in range(1, NZ):
            z_copy(c, step, True).start()
    turned = (((place >> 1) & 15) << 4) + ((place >> 5) << 1) + (place & 1)
    turn = jnp.where(turned == column, 1.0, 0.0).astype(bf)
    for c in range(CH):
        own = rows_of(z, 16)
        landed[c, own, :] = picked[c, own, :]
        for step in range(1, NZ):
            z_copy(c, step, False).wait_recv()
        out[:, c * CW : (c + 1) * CW] = mix(turn, landed[c]).astype(bf)

    for step in range(1, 8):
        q_copy(step).wait_send()
        for one in n_pair(step, True):
            one.wait_send()
        k_pair(step, True).wait_send()
        a_copy(step, True).wait_send()
        i_copy(step, True).wait_send()
        for c in range(CH):
            r_copy(c, step, True).wait_send()
            p_copy(c, step, True).wait_send()
    for step in range(1, NZ):
        for c in range(CH):
            z_copy(c, step, True).wait_send()
    for k in range(16):
        cond = o_remote(k)
        if cond is None:
            o_copy(k).wait_send()
        else:
            @pl.when(cond)
            def _():
                o_copy(k).wait_send()
    for dy in range(1, 4):
        m_copy(dy).wait_send()

    @pl.when(fs != y)
    def _():
        m_copy(0).wait_send()

    share(core, z, 0).wait_send()
    for way in range(2):
        for step in range(1, last[way] + 1):
            for stream in (q_ring, o_ring, m_ring):
                ring(*stream, way, step, False).wait_send()
            place_ = (z + NZ - step) % NZ if way == 0 else (z + step) % NZ
            share(core, place_, step + 8 * way).wait_send()


def block(*operands):
    bf = jnp.bfloat16
    dma = pltpu.SemaphoreType.DMA
    vm = pltpu.VMEM
    return pl.pallas_call(
        block_kernel,
        out_shape=jax.ShapeDtypeStruct((256, 1280), bf),
        in_specs=[pl.BlockSpec(memory_space=pltpu.VMEM)] * 8,
        out_specs=pl.BlockSpec(memory_space=pltpu.VMEM),
        scratch_shapes=[
            vm((NZ, 80, 512), bf), vm((2, NZ, 80, 640), bf), vm((NZ, 40, 1280), bf), vm((1280, 1280), bf),
            vm((1280, 128), bf), vm((8, 128, 1280), bf), vm((8, 8, 128), jnp.int32),
            vm((8, 16, 512), bf), vm((2, 8, 16, 384), bf), vm((4, 16, 1280), bf), vm((8, 8, 128), jnp.int32),
            vm((2, 512, 512), bf), vm((8, 160, 128), bf), vm((1280, 128), bf), vm((8, 32, 640), bf), vm((8, 32, 640), bf),
            vm((CH, 8, 32, CW), bf), vm((CH, 8, 32, CW), bf), vm((CH, 8, 32, CW), bf), vm((CH, 256, CW), bf), vm((CH, 256, CW), bf),
            dma((8,)), dma((8,)), dma((16,)), dma((2, 16)), dma((4,)), dma((4,)),
            dma((8,)), dma((8,)), dma((8,)), dma((8,)),
            dma((2, 8)), dma((2, 8)), dma((2, 8)), dma((2, 8)), dma((2, 8)), dma((2, 8)),
            dma((17,)), dma((17,)),
            dma((8,)), dma((8,)), dma((8,)), dma((8,)), dma((8,)), dma((8,)),
            dma((CH, 8)), dma((CH, 8)), dma((CH, 8)), dma((CH, 8)), dma((CH, NZ)), dma((CH, NZ)),
        ],
        compiler_params=pltpu.CompilerParams(collective_id=1, has_side_effects=True, vmem_limit_bytes=60 << 20),
    )(*operands)


def per_device(
    tokens, qkv_weight, out_weight, merge_weight, ln_gains, segments, merge_rows, owners
):
    fs = lax.axis_index("fsdp")
    y = lax.axis_index("yz") // NZ
    q_in = qkv_weight.reshape(3, 10, 2, 160).transpose(2, 1, 0, 3).reshape(2, 10, 480)
    q_in = jnp.pad(q_in, ((0, 0), (0, 6), (0, 32)))
    o_flat = out_weight.T
    o_in = jnp.where(fs % 2 == 0, jnp.pad(o_flat, ((0, 6), (0, 64))), jnp.pad(o_flat, ((0, 6), (64, 0))))
    m_in = jnp.pad(merge_weight, ((0, 6), (0, 0)))
    seg_in = jnp.broadcast_to(segments, (8, 128))
    order = merge_rows[0].reshape(32, 4).T.reshape(128, 1)
    order_in = jnp.broadcast_to(order, (128, 128))
    targets = owners[:, 0]
    ranks = jnp.arange(32)
    earlier = (targets[:, None] == targets[None, :]) & (ranks[None, :] < ranks[:, None])
    slot_row = targets * 2 + jnp.sum(earlier.astype(jnp.int32), axis=1) + 1
    spread = jnp.where(jnp.arange(4)[:, None] == y, slot_row[None, :], 0).reshape(1, 128)
    slot_in = jnp.broadcast_to(spread, (8, 128))
    return block(tokens, ln_gains, q_in, o_in, m_in, seg_in, order_in, slot_in)


def solution(mesh):
    cut = Mesh(mesh.devices.reshape(2, 64, 4), ("xh", "yz", "fsdp"))
    every = ("xh", "yz", "fsdp")
    return jax.shard_map(
        per_device,
        mesh=cut,
        in_specs=(
            P(every, None),
            P(None, ("xh", "yz"), "fsdp"),
            P("fsdp", ("xh", "yz")),
            P(every, None),
            P(),
            P(("xh", "yz"), "fsdp"),
            P(every, None),
            P(every, None),
        ),
        out_specs=P(every, None),
        check_vma=False,
    )
```

time: 752 us -> 158 us (0.21)
  the two profiles are of different devices: /device:TPU:24 before, /device:TPU:16 now
where the time goes in v3:
time: 158 us; the launch traced here: 157 us
  Pallas kernels  149 us (94%)
  local copies, waits for them, and re-layouts  6.55 us (4%)
  other arithmetic  1.62 us (1%)
    pallas_call x1, Pallas kernels, block(): pl.pallas_call(block_kernel, out_shape=jax.ShapeDtypeStruct((256, 1280),...  149 us

profile of v3, /device:TPU:16, one launch (start us, length us, event | category | flops | bytes accessed | tf_op | source)
XLA Modules:
  0.0 157.3 jit_solution(14890452240257985737)
XLA Ops:
  0.0 0.0 copy-start.4
  0.0 0.0 copy-start.5
  0.0 0.5 broadcast.36
  0.5 0.1 copy-done.4
  0.7 0.0 copy-start.2
  0.7 0.7 reduce.3
  1.3 0.0 copy-done.5
  1.3 0.2 convert_reduce_fusion
  1.5 0.1 broadcast_select_fusion
  1.6 0.1 select_n.35
  1.7 0.0 copy-start.3
  1.7 0.6 broadcast_in_dim.50.slot_in
  2.3 0.1 copy-done.3
  2.4 0.6 broadcast_in_dim.44.seg_in
  3.0 0.0 copy-done.2
  3.0 0.0 copy-start.1
  3.0 0.7 pad_select_fusion.o_in
  3.6 0.1 reshape_squeeze.3
  3.7 0.1 copy.16
  3.8 0.1 broadcast_in_dim.45
  3.9 0.0 copy-done.1
  3.9 0.1 reshape.39
  4.0 0.1 reshape.41
  4.1 0.0 copy-start
  4.2 0.6 pad.16.q_in
  4.8 0.2 copy-done
  4.9 0.6 pad.19.m_in
  5.6 0.7 broadcast_in_dim.46.order_in
  6.3 149.1 %shard_map.82 = bf16[256,1280]{1,0:T(8,128)(2,1)} custom-call(bf16[128,1280]{1,0:T(8,128)(2,1)} %tok_in.1, f32[2,1280]{1,0:T(2,128)} %gain_in.1, bf16[2,16,512]{2,1,0:T(8,128)(2,1)} %pad.16.q_in, bf16[16,384]{1,0:T(8,128)(2,1)} %pad_select_fusion.o_in, bf16[16,1280]{1,0:T(8,128)(2,1)} %pad.19.m_in, s32[8,128]{1,0:T(8,128)} %broadcast_in_dim.44.seg_in, ...), custom_call_target="tpu_custom_call" | custom-call | tf_op jit(solution)/shard_map/pallas_call | solution.py:450
  155.4 2.0 %copy.20 = bf16[256,1280]{1,0:T(8,128)(2,1)} copy(bf16[256,1280]{1,0:T(8,128)(2,1)} %shard_map.82) | data formatting | bytes 1310720
  (3 shorter events, 0.0 us)
Async XLA Ops:
  0.0 0.7 copy-start.4
  0.0 1.3 copy-start.5
  0.7 2.3 %copy-start.2 = (bf16[320,10]{0,1:T(8,128)(2,1)S(1)}, bf16[320,10]{0,1:T(8,128)(2,1)}, u32[]{:S(2)}) copy-start(bf16[320,10]{0,1:T(8,128)(2,1)} %param.10) | copy-start | bytes 19204
  1.7 0.7 copy-start.3
  3.0 0.9 copy-start.1
  4.1 0.8 copy-start

commit v4 on v3

--- a/solution.py
+++ b/solution.py
@@ -44,9 +44,9 @@
     tok_in, gain_in, q_in, o_in, m_in, seg_in, order_in, slot_in, out,
     wq, wo, wm, unmove, tok_t, normed_all, seg_all, q_box, o_box, m_box, slots,
     qkv, att_out, att_in, mi_out, mi_in, part_out, part_in, rows, picked, landed,
+    c_send, c_recv, y_send, y_recv, e_send, e_recv,
     q_send, q_recv, o_send, o_recv, m_send, m_recv, n_send, n_recv, g_send, g_recv,
-    zq_send, zq_recv, zo_send, zo_recv, zm_send, zm_recv, s_send, s_recv,
-    k_send, k_recv, a_send, a_recv, i_send, i_recv, r_send, r_recv, p_send, p_recv, z_send, z_recv,
+    s_send, s_recv, a_send, a_recv, i_send, i_recv, r_send, r_recv, p_send, p_recv,
 ):
     bf = jnp.bfloat16
     xh, y, z, fs = coords()
@@ -66,8 +66,8 @@
                 if dx or dy or df:
                     there = dev((xh + dx) % 2, (y + dy) % 4, z, (fs + df) % 4)
                     pl.semaphore_signal(barrier, inc=1, device_id=there, device_id_type=MESH)
-    for dz in range(1, NZ):
-        pl.semaphore_signal(barrier, inc=1, device_id=dev(xh, y, (z + dz) % NZ, fs), device_id_type=MESH)
+    for peer in (up, down):
+        pl.semaphore_signal(barrier, inc=1, device_id=dev(xh, y, peer, fs), device_id_type=MESH)
 
     lane = lax.broadcasted_iota(jnp.int32, (128, 128), 1)
     for b in range(10):
@@ -83,8 +83,8 @@
     normed = (center(tok_in[...].astype(jnp.float32)) * gain_in[0:1, :]).astype(bf)
     normed_all[member] = mix_t(normed, unmove[...]).astype(bf)
     seg_all[member] = seg_in[...]
-    slots[mine] = slot_in[...]
-    pl.semaphore_wait(barrier, 46)
+    slots[z] = slot_in[...]
+    pl.semaphore_wait(barrier, 33)
 
     def copy(src, dst, ssem, rsem, where):
         return pltpu.make_async_remote_copy(
@@ -157,29 +157,32 @@
         m_box[fs] = m_in[...]
 
 
-    def k_pair(step, to):
-        dx, dy = step // 4, step % 4
-        oxh = (xh + dx) % 2
-        oy = (y + dy) % 4 if to else (y + 4 - dy) % 4
-        slot = mine if to else oxh * 4 + oy
-        return copy(slot_in, slots.at[slot], k_send.at[step], k_recv.at[step], dev(oxh, oy, z, fs))
-
-    def n_pair(step, to):
+    sibling = dev(xh, y, z, xlo * 2 + 1 - core)
+    spot = xh * 2 + xlo
+
+    def n_copy(dx, to):
+        other = (spot + dx) % 4 if to else (spot + 4 - dx) % 4
+        oxh, ofs = other // 2, other % 2 * 2 + core
+        slot = member if to else oxh * 4 + ofs
+        return copy(normed_all.at[member], normed_all.at[slot], n_send.at[dx], n_recv.at[dx], dev(oxh, y, z, ofs))
+
+    def n_share(dx, to):
+        other = (spot + 4 - dx) % 4
+        slot = other // 2 * 4 + other % 2 * 2 + (core if to else 1 - core)
+        return copy(normed_all.at[slot], normed_all.at[slot], n_send.at[4 + dx], n_recv.at[4 + dx], sibling)
+
+    def g_copy(step, to):
         dx, df = step // 4, step % 4
         oxh = (xh + dx) % 2
         ofs = (fs + df) % 4 if to else (fs + 4 - df) % 4
         slot = member if to else oxh * 4 + ofs
-        there = dev(oxh, y, z, ofs)
-        return (
-            copy(normed_all.at[member], normed_all.at[slot], n_send.at[step], n_recv.at[step], there),
-            copy(seg_in, seg_all.at[slot], g_send.at[step], g_recv.at[step], there),
-        )
-
-    for step in range(1, 8):
-        for one in n_pair(step, True):
-            one.start()
-    for step in range(1, 8):
-        k_pair(step, True).start()
+        return copy(seg_in, seg_all.at[slot], g_send.at[step], g_recv.at[step], dev(oxh, y, z, ofs))
+
+    for dx in (1, 3, 2):
+        n_copy(dx, True).start()
+    n_share(0, True).start()
+    for step in range(1, 8):
+        g_copy(step, True).start()
 
     def ten(count, depth):
         place = lax.broadcasted_iota(jnp.int32, (count, depth), 0)
@@ -196,36 +199,74 @@
     wq[z] = settle(pick80, q_box[...].reshape(128, 512))
 
     last = (8, 7)
-
-    def ring(buf, ssem, rsem, way, step, arriving):
-        gone = step if arriving else step - 1
-        src = (z + NZ - gone) % NZ if way == 0 else (z + gone) % NZ
+    o_tile = y + y // 2
+    o_part = pl.ds(pl.multiple_of(o_tile * 128, 128), 128)
+    m_part = pl.ds(pl.multiple_of(y * 256, 256), 256)
+    views = (
+        lambda src: wq.at[src],
+        lambda src: wo.at[core, src, :, o_part],
+        lambda src: wo.at[core, src, :, pl.ds(256, 128)],
+        lambda src: wm.at[src, :, m_part],
+        lambda src: wm.at[src, :, pl.ds(1024, 256)],
+        lambda src: slots.at[src],
+    )
+
+    def block_at(way, gone):
+        return (z + NZ - gone) % NZ if way == 0 else (z + gone) % NZ
+
+    def ring(k, way, step, arriving):
+        view = views[k](block_at(way, step if arriving else step - 1))
         where = dev(xh, y, up if way == 0 else down, fs)
-        return copy(buf.at[src], buf.at[src], ssem.at[way, step - 1], rsem.at[way, step - 1], where)
-
-    q_ring = (wq, zq_send, zq_recv)
-    o_ring = (wo.at[core], zo_send, zo_recv)
-    m_ring = (wm, zm_send, zm_recv)
-    sibling = dev(xh, y, z, xlo * 2 + 1 - core)
+        return copy(view, view, c_send.at[k, way, step - 1], c_recv.at[k, way, step - 1], where)
+
+    def begin(k):
+        for way in range(2):
+            ring(k, way, 1, False).start()
 
     def share(half, place, slot):
         return copy(wo.at[half, place], wo.at[half, place], s_send.at[slot], s_recv.at[slot], sibling)
 
-    def begin(stream):
-        for way in range(2):
-            ring(*stream, way, 1, False).start()
-
-    def serve(stream, step):
-        for way in range(2):
-            if step <= last[way]:
-                ring(*stream, way, step, True).wait_recv()
-                if step < last[way]:
-                    ring(*stream, way, step + 1, False).start()
-                if stream is o_ring:
-                    place = (z + NZ - step) % NZ if way == 0 else (z + step) % NZ
-                    share(core, place, step + 8 * way).start()
-
-    begin(q_ring)
+    def o_along(place, slot, dy, to):
+        oy = (y + dy) % 4 if to else (y + 4 - dy) % 4
+        part = o_part if to else pl.ds(pl.multiple_of((oy + oy // 2) * 128, 128), 128)
+        view = wo.at[core, place, :, part]
+        return copy(view, view, y_send.at[slot, dy - 1], y_recv.at[slot, dy - 1], dev(xh, oy, z, fs))
+
+    def m_along(place, slot, dy, to):
+        oy = (y + dy) % 4 if to else (y + 4 - dy) % 4
+        part = m_part if to else pl.ds(pl.multiple_of(oy * 256, 256), 256)
+        view = wm.at[place, :, part]
+        return copy(view, view, y_send.at[slot, dy + 2], y_recv.at[slot, dy + 2], dev(xh, oy, z, fs))
+
+    def places(step):
+        if step == 0:
+            return [(z, 0)]
+        return [(block_at(way, step), step + 8 * way) for way in range(2) if step <= last[way]]
+
+    def serve(step):
+        for k in (0, 1, 3, 2, 4, 5):
+            for way in range(2):
+                if step <= last[way]:
+                    ring(k, way, step, True).wait_recv()
+                    if step < last[way]:
+                        ring(k, way, step + 1, False).start()
+
+    def spread_out(step):
+        for place, slot in places(step):
+            for dy in (1, 3, 2):
+                o_along(place, slot, dy, True).start()
+        for place, slot in places(step):
+            for dy in (1, 3, 2):
+                m_along(place, slot, dy, True).start()
+
+    def pass_on(step):
+        for place, slot in places(step):
+            for dy in range(1, 4):
+                o_along(place, slot, dy, False).wait_recv()
+            share(core, place, slot).start()
+
+    begin(0)
+    begin(5)
     for c in range(2):
         for k in range(16):
             dx, dl, dy = o_steps[k]
@@ -235,29 +276,38 @@
             @pl.when(cond)
             def _():
                 o_arrival(c, k).wait_recv()
-    left = o_box[0].reshape(128, 384)
-    right = o_box[1].reshape(128, 384)
-    wo[core, z, :, 0:256] = settle(pick80, left[:, 0:256])
-    wo[core, z, :, 256:384] = settle(pick80, left[:, 256:384] + right[:, 0:128])
-    wo[core, z, :, 384:640] = settle(pick80, right[:, 128:384])
-    begin(o_ring)
-    share(core, z, 0).start()
+    wo[core, z, :, 256:384] = settle(pick80, (o_box[0, :, :, 256:384] + o_box[1, :, :, 0:128]).reshape(128, 128))
+    from_lane = pl.ds(pl.multiple_of((y % 2 + y // 2) * 128, 128), 128)
+    wo[core, z, :, o_part] = settle(pick80, o_box[y // 2, :, :, from_lane].reshape(128, 128))
+    begin(1)
+    begin(2)
     for j in range(4):
         @pl.when((j != fs) | (y != fs))
         def _():
             m_arrival(j).wait_recv()
-    wm[z] = settle(ten(40, 64), m_box[...].reshape(64, 1280))
+    pick40 = ten(40, 64)
+    wm[z, :, m_part] = settle(pick40, m_box[:, :, m_part].reshape(64, 256))
+    wm[z, :, 1024:1280] = settle(pick40, m_box[:, :, 1024:1280].reshape(64, 256))
+    begin(3)
+    begin(4)
+    spread_out(0)
     tok_t[...] = mix_t(unmove[...], tok_in[...]).astype(bf)
 
     for step in range(1, 9):
-        serve(q_ring, step)
-        if step % 2 == 0:
-            serve(o_ring, step // 2)
+        serve(step)
+        spread_out(step)
+        pass_on(step - 1)
+        if step == 4:
+            for dx in (1, 3):
+                n_copy(dx, False).wait_recv()
+                n_share(dx, True).start()
         if step == 6:
-            begin(m_ring)
-    for step in range(1, 8):
-        for one in n_pair(step, False):
-            one.wait_recv()
+            n_copy(2, False).wait_recv()
+            n_share(2, True).start()
+    for dx in range(4):
+        n_share(dx, False).wait_recv()
+    for step in range(1, 8):
+        g_copy(step, False).wait_recv()
 
     factor = 1.0 / math.sqrt(HD)
 
@@ -294,26 +344,18 @@
                 att_out[g * 4 + b, h * HD : h * HD + HD, :] = head_out[:, b * 128 : (b + 1) * 128]
 
     project(0)
-    serve(o_ring, 5)
     attend(0)
-    serve(m_ring, 1)
     project(1)
-    serve(o_ring, 6)
     attend(1)
     att_in[rows_of(fs * 2 + xh, 160), :] = att_out[member]
     for step in range(1, 8):
         a_copy(step, True).start()
-    serve(m_ring, 2)
-    serve(o_ring, 7)
-    serve(m_ring, 3)
-    serve(o_ring, 8)
+    pass_on(8)
     for step in range(1, 8):
         a_copy(step, False).wait_recv()
-    share(1 - core, z, 0).wait_recv()
-    for way in range(2):
-        for step in range(1, last[way] + 1):
-            place = (z + NZ - step) % NZ if way == 0 else (z + step) % NZ
-            share(1 - core, place, step + 8 * way).wait_recv()
+    for step in range(9):
+        for place, slot in places(step):
+            share(1 - core, place, slot).wait_recv()
 
     update = mix(wo[0].reshape(1280, 640), att_in[0:640, :]) + mix(wo[1].reshape(1280, 640), att_in[640:1280, :])
     layer_t = (tok_t[...].astype(jnp.float32) + update).astype(bf)
@@ -334,8 +376,10 @@
     for step in range(1, 8):
         i_copy(step, True).start()
     mi_in[member] = mi_out[member]
-    for step in range(4, 9):
-        serve(m_ring, step)
+    for step in range(9):
+        for place, slot in places(step):
+            for dy in range(1, 4):
+                m_along(place, slot, dy, False).wait_recv()
     for step in range(1, 8):
         i_copy(step, False).wait_recv()
 
@@ -357,68 +401,67 @@
             r_copy(c, step, True).start()
         part_in[c, member] = part_out[c, member]
 
+    def e_copy(c, way, step, arriving):
+        view = rows.at[c, rows_of(block_at(way, step if arriving else step - 1), 32), :]
+        where = dev(xh, y, up if way == 0 else down, fs)
+        return copy(view, view, e_send.at[c, way, step - 1], e_recv.at[c, way, step - 1], where)
+
+    for c in range(CH):
+        for step in range(1, 8):
+            r_copy(c, step, False).wait_recv()
+        rows[c, rows_of(z, 32), :] = jnp.sum(part_in[c].astype(jnp.float32), axis=0).astype(bf)
+        for way in range(2):
+            e_copy(c, way, 1, False).start()
+
     def p_copy(c, step, to):
         dx, dy = step // 4, step % 4
         oxh = (xh + dx) % 2
         oy = (y + dy) % 4 if to else (y + 4 - dy) % 4
-        slot = mine if to else oxh * 4 + oy
+        other = oxh * 4 + oy
+        slot = mine if to else other
         return copy(
-            rows.at[c, mine], rows.at[c, slot], p_send.at[c, step], p_recv.at[c, step], dev(oxh, oy, z, fs)
+            picked.at[c, rows_of(other, 32), :], landed.at[c, rows_of(slot, 32), :],
+            p_send.at[c, step], p_recv.at[c, step], dev(oxh, oy, z, fs),
         )
 
-    for c in range(CH):
-        for step in range(1, 8):
-            r_copy(c, step, False).wait_recv()
-        rows[c, mine] = jnp.sum(part_in[c].astype(jnp.float32), axis=0).astype(bf)
-        for step in range(1, 8):
-            p_copy(c, step, True).start()
-
-    def z_copy(c, step, to):
-        other = (z + step) % NZ if to else (z + NZ - step) % NZ
-        slot = z if to else other
-        return copy(
-            picked.at[c, rows_of(other, 16), :], landed.at[c, rows_of(slot, 16), :],
-            z_send.at[c, step], z_recv.at[c, step], dev(xh, y, other, fs),
-        )
-
-    for step in range(1, 8):
-        k_pair(step, False).wait_recv()
     row_key = jnp.concatenate(
-        [slots[4 * q, 0:1, :] + slots[4 * q + 1, 0:1, :] + slots[4 * q + 2, 0:1, :] + slots[4 * q + 3, 0:1, :] for q in range(2)],
+        [slots[4 * q, 0:1, :] + slots[4 * q + 1, 0:1, :] + slots[4 * q + 2, 0:1, :] + slots[4 * q + 3, 0:1, :] for q in range(4)],
         axis=1,
     )
-    place = lax.broadcasted_iota(jnp.int32, (256, 256), 0)
-    column = lax.broadcasted_iota(jnp.int32, (256, 256), 1)
-    wanted = (mine * NZ + (place >> 4)) * 2 + (place & 1) + 1
-    select = jnp.where((((place >> 1) & 7) == (column >> 5)) & (row_key == wanted), 1.0, 0.0).astype(bf)
+    place = lax.broadcasted_iota(jnp.int32, (256, 512), 0)
+    column = lax.broadcasted_iota(jnp.int32, (256, 512), 1)
+    wanted = (place & 224) + 2 * z + (place & 1) + 1
+    select = jnp.where((((place >> 1) & 15) == (column >> 5)) & (row_key == wanted), 1.0, 0.0).astype(bf)
+    for step in range(1, 9):
+        for c in range(CH):
+            for way in range(2):
+                if step <= last[way]:
+                    e_copy(c, way, step, True).wait_recv()
+                    if step < last[way]:
+                        e_copy(c, way, step + 1, False).start()
+            if step == 8:
+                picked[c] = mix(select, rows[c]).astype(bf)
+                for hop in range(1, 8):
+                    p_copy(c, hop, True).start()
+    own = rows_of(mine, 32)
     for c in range(CH):
+        landed[c, own, :] = picked[c, own, :]
         for step in range(1, 8):
             p_copy(c, step, False).wait_recv()
-        picked[c] = mix(select, rows[c].reshape(256, CW)).astype(bf)
-        for step in range(1, NZ):
-            z_copy(c, step, True).start()
-    turned = (((place >> 1) & 15) << 4) + ((place >> 5) << 1) + (place & 1)
-    turn = jnp.where(turned == column, 1.0, 0.0).astype(bf)
-    for c in range(CH):
-        own = rows_of(z, 16)
-        landed[c, own, :] = picked[c, own, :]
-        for step in range(1, NZ):
-            z_copy(c, step, False).wait_recv()
-        out[:, c * CW : (c + 1) * CW] = mix(turn, landed[c]).astype(bf)
+        out[:, c * CW : (c + 1) * CW] = landed[c]
 
     for step in range(1, 8):
         q_copy(step).wait_send()
-        for one in n_pair(step, True):
-            one.wait_send()
-        k_pair(step, True).wait_send()
+        g_copy(step, True).wait_send()
         a_copy(step, True).wait_send()
         i_copy(step, True).wait_send()
         for c in range(CH):
             r_copy(c, step, True).wait_send()
             p_copy(c, step, True).wait_send()
-    for step in range(1, NZ):
-        for c in range(CH):
-            z_copy(c, step, True).wait_send()
+    for dx in range(4):
+        n_share(dx, True).wait_send()
+        if dx:
+            n_copy(dx, True).wait_send()
     for k in range(16):
         cond = o_remote(k)
         if cond is None:
@@ -434,13 +477,18 @@
     def _():
         m_copy(0).wait_send()
 
-    share(core, z, 0).wait_send()
     for way in range(2):
         for step in range(1, last[way] + 1):
-            for stream in (q_ring, o_ring, m_ring):
-                ring(*stream, way, step, False).wait_send()
-            place_ = (z + NZ - step) % NZ if way == 0 else (z + step) % NZ
-            share(core, place_, step + 8 * way).wait_send()
+            for k in range(6):
+                ring(k, way, step, False).wait_send()
+            for c in range(CH):
+                e_copy(c, way, step, False).wait_send()
+    for step in range(9):
+        for place_, slot in places(step):
+            share(core, place_, slot).wait_send()
+            for dy in range(1, 4):
+                o_along(place_, slot, dy, True).wait_send()
+                m_along(place_, slot, dy, True).wait_send()
 
 
 def block(*operands):
@@ -455,15 +503,14 @@
         scratch_shapes=[
             vm((NZ, 80, 512), bf), vm((2, NZ, 80, 640), bf), vm((NZ, 40, 1280), bf), vm((1280, 1280), bf),
             vm((1280, 128), bf), vm((8, 128, 1280), bf), vm((8, 8, 128), jnp.int32),
-            vm((8, 16, 512), bf), vm((2, 8, 16, 384), bf), vm((4, 16, 1280), bf), vm((8, 8, 128), jnp.int32),
+            vm((8, 16, 512), bf), vm((2, 8, 16, 384), bf), vm((4, 16, 1280), bf), vm((NZ, 8, 128), jnp.int32),
             vm((2, 512, 512), bf), vm((8, 160, 128), bf), vm((1280, 128), bf), vm((8, 32, 640), bf), vm((8, 32, 640), bf),
-            vm((CH, 8, 32, CW), bf), vm((CH, 8, 32, CW), bf), vm((CH, 8, 32, CW), bf), vm((CH, 256, CW), bf), vm((CH, 256, CW), bf),
+            vm((CH, 8, 32, CW), bf), vm((CH, 8, 32, CW), bf), vm((CH, 512, CW), bf), vm((CH, 256, CW), bf), vm((CH, 256, CW), bf),
+            dma((6, 2, 8)), dma((6, 2, 8)), dma((17, 6)), dma((17, 6)), dma((CH, 2, 8)), dma((CH, 2, 8)),
             dma((8,)), dma((8,)), dma((16,)), dma((2, 16)), dma((4,)), dma((4,)),
             dma((8,)), dma((8,)), dma((8,)), dma((8,)),
-            dma((2, 8)), dma((2, 8)), dma((2, 8)), dma((2, 8)), dma((2, 8)), dma((2, 8)),
-            dma((17,)), dma((17,)),
-            dma((8,)), dma((8,)), dma((8,)), dma((8,)), dma((8,)), dma((8,)),
-            dma((CH, 8)), dma((CH, 8)), dma((CH, 8)), dma((CH, 8)), dma((CH, NZ)), dma((CH, NZ)),
+            dma((17,)), dma((17,)), dma((8,)), dma((8,)), dma((8,)), dma((8,)),
+            dma((CH, 8)), dma((CH, 8)), dma((CH, 8)), dma((CH, 8)),
         ],
         compiler_params=pltpu.CompilerParams(collective_id=1, has_side_effects=True, vmem_limit_bytes=60 << 20),
     )(*operands)
@@ -473,7 +520,7 @@
     tokens, qkv_weight, out_weight, merge_weight, ln_gains, segments, merge_rows, owners
 ):
     fs = lax.axis_index("fsdp")
-    y = lax.axis_index("yz") // NZ
+    z = lax.axis_index("yz") % NZ
     q_in = qkv_weight.reshape(3, 10, 2, 160).transpose(2, 1, 0, 3).reshape(2, 10, 480)
     q_in = jnp.pad(q_in, ((0, 0), (0, 6), (0, 32)))
     o_flat = out_weight.T
@@ -486,7 +533,7 @@
     ranks = jnp.arange(32)
     earlier = (targets[:, None] == targets[None, :]) & (ranks[None, :] < ranks[:, None])
     slot_row = targets * 2 + jnp.sum(earlier.astype(jnp.int32), axis=1) + 1
-    spread = jnp.where(jnp.arange(4)[:, None] == y, slot_row[None, :], 0).reshape(1, 128)
+    spread = jnp.where(jnp.arange(4)[:, None] == z % 4, slot_row[None, :], 0).reshape(1, 128)
     slot_in = jnp.broadcast_to(spread, (8, 128))
     return block(tokens, ln_gains, q_in, o_in, m_in, seg_in, order_in, slot_in)
 

time: 158 us -> 133 us (0.84)
  the two profiles are of different devices: /device:TPU:16 before, /device:TPU:24 now
where the time goes in v4:
time: 133 us; the launch traced here: 131 us
  Pallas kernels  123 us (92%)
  local copies, waits for them, and re-layouts  6.55 us (5%)
  other arithmetic  1.62 us (1%)
    pallas_call x1, Pallas kernels, block(): pl.pallas_call(block_kernel, out_shape=jax.ShapeDtypeStruct((256, 1280),...  123 us
    unnamed x14, local copies, waits for them, and re-layouts  2.85 us

profile of v4, /device:TPU:24, one launch (start us, length us, event | category | flops | bytes accessed | tf_op | source)
XLA Modules:
  0.0 131.2 jit_solution(4205341787950581194)
XLA Ops:
  0.0 0.0 copy-start.4
  0.0 0.0 copy-start.5
  0.0 0.5 broadcast.37
  0.5 0.1 copy-done.4
  0.7 0.0 copy-start.2
  0.7 0.7 reduce.3
  1.3 0.0 copy-done.5
  1.3 0.2 convert_reduce_fusion
  1.5 0.1 broadcast_select_fusion
  1.6 0.1 select_n.40
  1.7 0.0 copy-start.3
  1.7 0.6 broadcast_in_dim.50.slot_in
  2.3 0.1 copy-done.3
  2.4 0.6 broadcast_in_dim.44.seg_in
  3.0 0.0 copy-done.2
  3.0 0.0 copy-start.1
  3.0 0.7 pad_select_fusion.o_in
  3.6 0.1 reshape_squeeze.3
  3.7 0.1 copy.16
  3.8 0.1 broadcast_in_dim.45
  3.9 0.0 copy-done.1
  3.9 0.1 reshape.39
  4.0 0.1 reshape.41
  4.1 0.0 copy-start
  4.2 0.6 pad.16.q_in
  4.8 0.2 copy-done
  4.9 0.6 pad.19.m_in
  5.6 0.7 broadcast_in_dim.46.order_in
  6.3 122.9 %shard_map.82 = bf16[256,1280]{1,0:T(8,128)(2,1)} custom-call(bf16[128,1280]{1,0:T(8,128)(2,1)} %tok_in.1, f32[2,1280]{1,0:T(2,128)} %gain_in.1, bf16[2,16,512]{2,1,0:T(8,128)(2,1)} %pad.16.q_in, bf16[16,384]{1,0:T(8,128)(2,1)} %pad_select_fusion.o_in, bf16[16,1280]{1,0:T(8,128)(2,1)} %pad.19.m_in, s32[8,128]{1,0:T(8,128)} %broadcast_in_dim.44.seg_in, ...), custom_call_target="tpu_custom_call" | custom-call | tf_op jit(solution)/shard_map/pallas_call | solution.py:498
  129.2 2.0 %copy.20 = bf16[256,1280]{1,0:T(8,128)(2,1)} copy(bf16[256,1280]{1,0:T(8,128)(2,1)} %shard_map.82) | data formatting | bytes 1310720
  (3 shorter events, 0.0 us)
Async XLA Ops:
  0.0 0.7 copy-start.4
  0.0 1.3 %copy-start.5 = (s32[32,1]{0,1:T(1,128)S(1)}, s32[32,1]{0,1:T(1,128)}, u32[]{:S(2)}) copy-start(s32[32,1]{0,1:T(1,128)} %param.15) | copy-start | bytes 388
  0.7 2.3 %copy-start.2 = (bf16[320,10]{0,1:T(8,128)(2,1)S(1)}, bf16[320,10]{0,1:T(8,128)(2,1)}, u32[]{:S(2)}) copy-start(bf16[320,10]{0,1:T(8,128)(2,1)} %param.10) | copy-start | bytes 19204
  1.7 0.7 copy-start.3
  3.0 0.9 copy-start.1
  4.1 0.8 copy-start

commit v5 on v4

--- a/solution.py
+++ b/solution.py
@@ -41,9 +41,9 @@
 
 
 def block_kernel(
-    tok_in, gain_in, q_in, o_in, m_in, seg_in, order_in, slot_in, out,
+    tok_in, gain_in, q_in, o_in, m_in, seg_row, order_row, owner_col, out, seg_in,
     wq, wo, wm, unmove, tok_t, normed_all, seg_all, q_box, o_box, m_box, slots,
-    qkv, att_out, att_in, mi_out, mi_in, part_out, part_in, rows, picked, landed,
+    qkv, att_out, att_in, mi_out, mi_in, part_out, part_in, rows, picked1, picked2, picked3, landed1, landed2, landed3,
     c_send, c_recv, y_send, y_recv, e_send, e_recv,
     q_send, q_recv, o_send, o_recv, m_send, m_recv, n_send, n_recv, g_send, g_recv,
     s_send, s_recv, a_send, a_recv, i_send, i_recv, r_send, r_recv, p_send, p_recv,
@@ -54,7 +54,7 @@
     xlo = fs // 2
     mine = xh * 4 + y
     member = xh * 4 + fs
-    up, down = (z + 1) % NZ, (z + NZ - 1) % NZ
+    up, below = (z + 1) % NZ, (z + NZ - 1) % NZ
 
     def dev(xh_, y_, z_, fs_):
         return (xh_, y_ * NZ + z_, fs_)
@@ -66,7 +66,7 @@
                 if dx or dy or df:
                     there = dev((xh + dx) % 2, (y + dy) % 4, z, (fs + df) % 4)
                     pl.semaphore_signal(barrier, inc=1, device_id=there, device_id_type=MESH)
-    for peer in (up, down):
+    for peer in (up, below):
         pl.semaphore_signal(barrier, inc=1, device_id=dev(xh, y, peer, fs), device_id_type=MESH)
 
     lane = lax.broadcasted_iota(jnp.int32, (128, 128), 1)
@@ -82,8 +82,16 @@
             ).astype(bf)
     normed = (center(tok_in[...].astype(jnp.float32)) * gain_in[0:1, :]).astype(bf)
     normed_all[member] = mix_t(normed, unmove[...]).astype(bf)
+    seg_in[...] = jnp.broadcast_to(seg_row[...], (8, 128))
     seg_all[member] = seg_in[...]
-    slots[z] = slot_in[...]
+    down_owner = jnp.broadcast_to(owner_col[...], (32, 128)).astype(jnp.float32)
+    over_owner = jnp.concatenate([down_owner] * 4, axis=0).T
+    over_owner = jnp.concatenate([over_owner[0:32, 0:32]] * 4, axis=1)
+    lane32 = lax.broadcasted_iota(jnp.int32, (32, 128), 1) & 31
+    earlier = (down_owner == over_owner) & (lax.broadcasted_iota(jnp.int32, (32, 128), 0) < lane32)
+    rank = jnp.sum(jnp.where(earlier, 1.0, 0.0), axis=0, keepdims=True)
+    slot_row = (over_owner[0:1, :] * 2.0 + rank + 1.0).astype(jnp.int32)
+    slots[z] = jnp.broadcast_to(slot_row, (8, 128))
     pl.semaphore_wait(barrier, 33)
 
     def copy(src, dst, ssem, rsem, where):
@@ -140,22 +148,33 @@
         o_box[core, mine] = o_in[...]
 
     def m_copy(dy):
-        return copy(m_in, m_box.at[fs], m_send.at[dy], m_recv.at[fs], dev(xh, (y + dy) % 4, z, y))
+        oy = (y + dy) % 4
+        there = dev(xh, oy, z, y)
+        return (
+            copy(m_in.at[:, pl.ds(pl.multiple_of(oy * 256, 256), 256)], m_box.at[0, fs], m_send.at[0, dy], m_recv.at[0, fs], there),
+            copy(m_in.at[:, pl.ds(1024, 256)], m_box.at[1, fs], m_send.at[1, dy], m_recv.at[1, fs], there),
+        )
 
     def m_arrival(j):
-        return copy(m_in, m_box.at[j], m_send.at[0], m_recv.at[j], dev(xh, fs, z, j))
+        there = dev(xh, fs, z, j)
+        return [
+            copy(m_in.at[:, pl.ds(1024, 256)], m_box.at[half, j], m_send.at[half, 0], m_recv.at[half, j], there)
+            for half in range(2)
+        ]
 
     for dy in range(1, 4):
-        m_copy(dy).start()
+        for one in m_copy(dy):
+            one.start()
 
     @pl.when(fs != y)
     def _():
-        m_copy(0).start()
+        for one in m_copy(0):
+            one.start()
 
     @pl.when(fs == y)
     def _():
-        m_box[fs] = m_in[...]
-
+        m_box[0, fs] = m_in[:, pl.ds(pl.multiple_of(y * 256, 256), 256)]
+        m_box[1, fs] = m_in[:, 1024:1280]
 
     sibling = dev(xh, y, z, xlo * 2 + 1 - core)
     spot = xh * 2 + xlo
@@ -216,7 +235,7 @@
 
     def ring(k, way, step, arriving):
         view = views[k](block_at(way, step if arriving else step - 1))
-        where = dev(xh, y, up if way == 0 else down, fs)
+        where = dev(xh, y, up if way == 0 else below, fs)
         return copy(view, view, c_send.at[k, way, step - 1], c_recv.at[k, way, step - 1], where)
 
     def begin(k):
@@ -284,10 +303,11 @@
     for j in range(4):
         @pl.when((j != fs) | (y != fs))
         def _():
-            m_arrival(j).wait_recv()
+            for one in m_arrival(j):
+                one.wait_recv()
     pick40 = ten(40, 64)
-    wm[z, :, m_part] = settle(pick40, m_box[:, :, m_part].reshape(64, 256))
-    wm[z, :, 1024:1280] = settle(pick40, m_box[:, :, 1024:1280].reshape(64, 256))
+    wm[z, :, m_part] = settle(pick40, m_box[0].reshape(64, 256))
+    wm[z, :, 1024:1280] = settle(pick40, m_box[1].reshape(64, 256))
     begin(3)
     begin(4)
     spread_out(0)
@@ -321,20 +341,17 @@
         )
 
     def project(g):
-        block = normed_all[g * 4 : (g + 1) * 4].reshape(512, 1280)
-        qkv[g] = mix(block, wq[...].reshape(1280, 512)).astype(bf)
+        block = normed_all[pl.ds(g * 4, 4)].reshape(512, 1280)
+        qkv[...] = mix(block, wq[...].reshape(1280, 512)).astype(bf)
 
     def attend(g):
-        across = jnp.concatenate([seg_all[g * 4 + b, 0:1, :] for b in range(4)], axis=1)
-        downs = []
-        for b in range(4):
-            one = jnp.broadcast_to(seg_all[g * 4 + b, 0:1, :].astype(jnp.float32), (128, 128)).T
-            downs.append(jnp.concatenate([one] * 4, axis=1))
-        allowed = jnp.concatenate(downs, axis=0) == across.astype(jnp.float32)
+        names = [seg_all[g * 4 + b][0:1, :].astype(jnp.float32) for b in range(4)]
+        downs = [jnp.concatenate([jnp.broadcast_to(one, (128, 128)).T] * 4, axis=1) for one in names]
+        allowed = jnp.concatenate(downs, axis=0) == jnp.concatenate(names, axis=1)
         for h in range(2):
-            query = qkv[g, :, h * HD : h * HD + HD]
-            key = qkv[g, :, 160 + h * HD : 160 + h * HD + HD]
-            value = qkv[g, :, 320 + h * HD : 320 + h * HD + HD]
+            query = qkv[:, h * HD : h * HD + HD]
+            key = qkv[:, 160 + h * HD : 160 + h * HD + HD]
+            value = qkv[:, 320 + h * HD : 320 + h * HD + HD]
             scores = jnp.where(allowed, mix_t(key, query) * factor, -jnp.inf)
             weights = jnp.exp(scores - jnp.max(scores, axis=0, keepdims=True))
             totals = jnp.sum(weights, axis=0, keepdims=True)
@@ -343,12 +360,14 @@
             for b in range(4):
                 att_out[g * 4 + b, h * HD : h * HD + HD, :] = head_out[:, b * 128 : (b + 1) * 128]
 
-    project(0)
-    attend(0)
-    project(1)
-    attend(1)
+    project(1 - xh)
+    attend(1 - xh)
+    for step in range(4, 8):
+        a_copy(step, True).start()
+    project(xh)
+    attend(xh)
     att_in[rows_of(fs * 2 + xh, 160), :] = att_out[member]
-    for step in range(1, 8):
+    for step in range(1, 4):
         a_copy(step, True).start()
     pass_on(8)
     for step in range(1, 8):
@@ -359,7 +378,10 @@
 
     update = mix(wo[0].reshape(1280, 640), att_in[0:640, :]) + mix(wo[1].reshape(1280, 640), att_in[640:1280, :])
     layer_t = (tok_t[...].astype(jnp.float32) + update).astype(bf)
-    picker = jnp.where(order_in[...] == lane, 1.0, 0.0).astype(bf)
+    down = lax.broadcasted_iota(jnp.int32, (128, 128), 0)
+    named = jnp.where(order_row[...] == down, 1.0, 0.0).astype(bf)
+    regular = jnp.where(lane == ((down & 31) << 2) + (down >> 5), 1.0, 0.0).astype(bf)
+    picker = mix_t(regular, named).astype(bf)
     chosen = mix_t(picker, layer_t).astype(bf)
     merge_in = (center(mix(chosen, unmove[...])) * gain_in[1:2, :]).astype(bf)
     for b in range(8):
@@ -401,54 +423,95 @@
             r_copy(c, step, True).start()
         part_in[c, member] = part_out[c, member]
 
-    def e_copy(c, way, step, arriving):
-        view = rows.at[c, rows_of(block_at(way, step if arriving else step - 1), 32), :]
-        where = dev(xh, y, up if way == 0 else down, fs)
-        return copy(view, view, e_send.at[c, way, step - 1], e_recv.at[c, way, step - 1], where)
+    def seat(way, gone):
+        return 0 if gone == 0 else 15 if gone == 8 else 2 * gone - 1 + way
+
+    def e_copy(c, way, step):
+        where = dev(xh, y, up if way == 0 else below, fs)
+        return copy(
+            rows.at[c, seat(way, step - 1)], rows.at[c, seat(way, step)], e_send.at[c, way, step - 1], e_recv.at[c, way, step - 1], where
+        )
 
     for c in range(CH):
         for step in range(1, 8):
             r_copy(c, step, False).wait_recv()
-        rows[c, rows_of(z, 32), :] = jnp.sum(part_in[c].astype(jnp.float32), axis=0).astype(bf)
+        rows[c, 0] = jnp.sum(part_in[c].astype(jnp.float32), axis=0).astype(bf)
         for way in range(2):
-            e_copy(c, way, 1, False).start()
-
-    def p_copy(c, step, to):
+            e_copy(c, way, 1).start()
+
+    parts = ((0, 8, 4), (8, 4, 6), (12, 4, 8))
+    boxes = ((picked1, landed1), (picked2, landed2), (picked3, landed3))
+
+    def p_copy(part, c, step, to):
         dx, dy = step // 4, step % 4
         oxh = (xh + dx) % 2
         oy = (y + dy) % 4 if to else (y + 4 - dy) % 4
         other = oxh * 4 + oy
         slot = mine if to else other
+        gone, come = boxes[part]
         return copy(
-            picked.at[c, rows_of(other, 32), :], landed.at[c, rows_of(slot, 32), :],
-            p_send.at[c, step], p_recv.at[c, step], dev(oxh, oy, z, fs),
+            gone.at[c, other], come.at[c, slot], p_send.at[part, c, step], p_recv.at[part, c, step], dev(oxh, oy, z, fs)
         )
 
-    row_key = jnp.concatenate(
-        [slots[4 * q, 0:1, :] + slots[4 * q + 1, 0:1, :] + slots[4 * q + 2, 0:1, :] + slots[4 * q + 3, 0:1, :] for q in range(4)],
-        axis=1,
-    )
-    place = lax.broadcasted_iota(jnp.int32, (256, 512), 0)
-    column = lax.broadcasted_iota(jnp.int32, (256, 512), 1)
-    wanted = (place & 224) + 2 * z + (place & 1) + 1
-    select = jnp.where((((place >> 1) & 15) == (column >> 5)) & (row_key == wanted), 1.0, 0.0).astype(bf)
+    row_keys = []
+    lane_row = lax.broadcasted_iota(jnp.int32, (1, 128), 1)
+    for q in range(4):
+        row_key = jnp.zeros((1, 128), jnp.int32)
+        for i in range(4):
+            number = 4 * q + i
+            gone = (number + 1) // 2
+            source = block_at(0, gone) if number % 2 else block_at(1, gone)
+            row_key = jnp.where((lane_row >> 5) == i, slots[source][0:1, :], row_key)
+        row_keys.append(row_key)
+    selects, turns = [], []
+    for first, count, _ in parts:
+        shape = (16 * count, 32 * count)
+        bits = 4 if count == 8 else 3
+        place = lax.broadcasted_iota(jnp.int32, shape, 0)
+        column = lax.broadcasted_iota(jnp.int32, shape, 1)
+        wanted = ((place >> bits) << 5) + 2 * z + (place & 1) + 1
+        keys = jnp.concatenate(row_keys[first // 4 : (first + count) // 4], axis=1)
+        match = (((place >> 1) & (count - 1)) == (column >> 5)) & (keys == wanted)
+        selects.append(jnp.where(match, 1.0, 0.0).astype(bf))
+        shape = (256, 16 * count)
+        place = lax.broadcasted_iota(jnp.int32, shape, 0)
+        column = lax.broadcasted_iota(jnp.int32, shape, 1)
+        number = ((column >> 1) & (count - 1)) + first
+        gone = (number + 1) >> 1
+        source = (z + jnp.where((number & 1) == 1, NZ - gone, gone)) & 15
+        match = ((place >> 5) == (column >> bits)) & ((place & 1) == (column & 1)) & (((place >> 1) & 15) == source)
+        turns.append(jnp.where(match, 1.0, 0.0).astype(bf))
     for step in range(1, 9):
         for c in range(CH):
             for way in range(2):
                 if step <= last[way]:
-                    e_copy(c, way, step, True).wait_recv()
+                    e_copy(c, way, step).wait_recv()
                     if step < last[way]:
-                        e_copy(c, way, step + 1, False).start()
+                        e_copy(c, way, step + 1).start()
             if step == 8:
-                picked[c] = mix(select, rows[c]).astype(bf)
+                first, count, _ = parts[2]
+                block = mix(selects[2], rows[c, first : first + count].reshape(32 * count, CW)).astype(bf)
+                boxes[2][0][c] = block.reshape(8, 2 * count, CW)
                 for hop in range(1, 8):
-                    p_copy(c, hop, True).start()
-    own = rows_of(mine, 32)
+                    p_copy(2, c, hop, True).start()
+        for part in range(2):
+            first, count, ready = parts[part]
+            if step == ready:
+                for c in range(CH):
+                    block = mix(selects[part], rows[c, first : first + count].reshape(32 * count, CW)).astype(bf)
+                    boxes[part][0][c] = block.reshape(8, 2 * count, CW)
+                    for hop in range(1, 8):
+                        p_copy(part, c, hop, True).start()
     for c in range(CH):
-        landed[c, own, :] = picked[c, own, :]
-        for step in range(1, 8):
-            p_copy(c, step, False).wait_recv()
-        out[:, c * CW : (c + 1) * CW] = landed[c]
+        total = None
+        for part in range(3):
+            gone, come = boxes[part]
+            come[c, mine] = gone[c, mine]
+            for step in range(1, 8):
+                p_copy(part, c, step, False).wait_recv()
+            block = mix(turns[part], come[c].reshape(16 * parts[part][1], CW))
+            total = block if total is None else total + block
+        out[:, c * CW : (c + 1) * CW] = total.astype(bf)
 
     for step in range(1, 8):
         q_copy(step).wait_send()
@@ -457,7 +520,8 @@
         i_copy(step, True).wait_send()
         for c in range(CH):
             r_copy(c, step, True).wait_send()
-            p_copy(c, step, True).wait_send()
+            for part in range(3):
+                p_copy(part, c, step, True).wait_send()
     for dx in range(4):
         n_share(dx, True).wait_send()
         if dx:
@@ -471,18 +535,20 @@
             def _():
                 o_copy(k).wait_send()
     for dy in range(1, 4):
-        m_copy(dy).wait_send()
+        for one in m_copy(dy):
+            one.wait_send()
 
     @pl.when(fs != y)
     def _():
-        m_copy(0).wait_send()
+        for one in m_copy(0):
+            one.wait_send()
 
     for way in range(2):
         for step in range(1, last[way] + 1):
             for k in range(6):
                 ring(k, way, step, False).wait_send()
             for c in range(CH):
-                e_copy(c, way, step, False).wait_send()
+                e_copy(c, way, step).wait_send()
     for step in range(9):
         for place_, slot in places(step):
             share(core, place_, slot).wait_send()
@@ -501,16 +567,17 @@
         in_specs=[pl.BlockSpec(memory_space=pltpu.VMEM)] * 8,
         out_specs=pl.BlockSpec(memory_space=pltpu.VMEM),
         scratch_shapes=[
-            vm((NZ, 80, 512), bf), vm((2, NZ, 80, 640), bf), vm((NZ, 40, 1280), bf), vm((1280, 1280), bf),
+            vm((8, 128), jnp.int32), vm((NZ, 80, 512), bf), vm((2, NZ, 80, 640), bf), vm((NZ, 40, 1280), bf), vm((1280, 1280), bf),
             vm((1280, 128), bf), vm((8, 128, 1280), bf), vm((8, 8, 128), jnp.int32),
-            vm((8, 16, 512), bf), vm((2, 8, 16, 384), bf), vm((4, 16, 1280), bf), vm((NZ, 8, 128), jnp.int32),
-            vm((2, 512, 512), bf), vm((8, 160, 128), bf), vm((1280, 128), bf), vm((8, 32, 640), bf), vm((8, 32, 640), bf),
-            vm((CH, 8, 32, CW), bf), vm((CH, 8, 32, CW), bf), vm((CH, 512, CW), bf), vm((CH, 256, CW), bf), vm((CH, 256, CW), bf),
+            vm((8, 16, 512), bf), vm((2, 8, 16, 384), bf), vm((2, 4, 16, 256), bf), vm((NZ, 8, 128), jnp.int32),
+            vm((512, 512), bf), vm((8, 160, 128), bf), vm((1280, 128), bf), vm((8, 32, 640), bf), vm((8, 32, 640), bf),
+            vm((CH, 8, 32, CW), bf), vm((CH, 8, 32, CW), bf), vm((CH, NZ, 32, CW), bf),
+            vm((CH, 8, 16, CW), bf), vm((CH, 8, 8, CW), bf), vm((CH, 8, 8, CW), bf), vm((CH, 8, 16, CW), bf), vm((CH, 8, 8, CW), bf), vm((CH, 8, 8, CW), bf),
             dma((6, 2, 8)), dma((6, 2, 8)), dma((17, 6)), dma((17, 6)), dma((CH, 2, 8)), dma((CH, 2, 8)),
-            dma((8,)), dma((8,)), dma((16,)), dma((2, 16)), dma((4,)), dma((4,)),
+            dma((8,)), dma((8,)), dma((16,)), dma((2, 16)), dma((2, 4)), dma((2, 4)),
             dma((8,)), dma((8,)), dma((8,)), dma((8,)),
             dma((17,)), dma((17,)), dma((8,)), dma((8,)), dma((8,)), dma((8,)),
-            dma((CH, 8)), dma((CH, 8)), dma((CH, 8)), dma((CH, 8)),
+            dma((CH, 8)), dma((CH, 8)), dma((3, CH, 8)), dma((3, CH, 8)),
         ],
         compiler_params=pltpu.CompilerParams(collective_id=1, has_side_effects=True, vmem_limit_bytes=60 << 20),
     )(*operands)
@@ -520,22 +587,12 @@
     tokens, qkv_weight, out_weight, merge_weight, ln_gains, segments, merge_rows, owners
 ):
     fs = lax.axis_index("fsdp")
-    z = lax.axis_index("yz") % NZ
     q_in = qkv_weight.reshape(3, 10, 2, 160).transpose(2, 1, 0, 3).reshape(2, 10, 480)
     q_in = jnp.pad(q_in, ((0, 0), (0, 6), (0, 32)))
     o_flat = out_weight.T
     o_in = jnp.where(fs % 2 == 0, jnp.pad(o_flat, ((0, 6), (0, 64))), jnp.pad(o_flat, ((0, 6), (64, 0))))
     m_in = jnp.pad(merge_weight, ((0, 6), (0, 0)))
-    seg_in = jnp.broadcast_to(segments, (8, 128))
-    order = merge_rows[0].reshape(32, 4).T.reshape(128, 1)
-    order_in = jnp.broadcast_to(order, (128, 128))
-    targets = owners[:, 0]
-    ranks = jnp.arange(32)
-    earlier = (targets[:, None] == targets[None, :]) & (ranks[None, :] < ranks[:, None])
-    slot_row = targets * 2 + jnp.sum(earlier.astype(jnp.int32), axis=1) + 1
-    spread = jnp.where(jnp.arange(4)[:, None] == z % 4, slot_row[None, :], 0).reshape(1, 128)
-    slot_in = jnp.broadcast_to(spread, (8, 128))
-    return block(tokens, ln_gains, q_in, o_in, m_in, seg_in, order_in, slot_in)
+    return block(tokens, ln_gains, q_in, o_in, m_in, segments, merge_rows, owners)
 
 
 def solution(mesh):

time: 133 us -> 128 us (0.962)
  Pallas kernels: 123 us -> 121 us
  local copies, waits for them, and re-layouts: 6.55 us -> 4.98 us
    pallas_call x1, Pallas kernels: 123 us -> 121 us  [block(): pl.pallas_call(block_kernel, out_shape=jax.ShapeDtypeStruct((256, 1280),...]
    broadcast_in_dim x4 -> x0, local copies, waits for them, and re-layouts: 1.99 us -> none  [the longest x2 0.8 us: per_device(): order_in = jnp.broadcast_to(order, (128, 128))]
    unnamed x14 -> x10, local copies, waits for them, and re-layouts: 2.85 us -> 3.53 us
where the time goes in v5:
time: 128 us; the launch traced here: 126 us
  Pallas kernels  121 us (95%)
  local copies, waits for them, and re-layouts  4.98 us (4%)
    pallas_call x1, Pallas kernels, block(): pl.pallas_call(block_kernel, out_shape=jax.ShapeDtypeStruct((256, 1280),...  121 us
    unnamed x10, local copies, waits for them, and re-layouts  3.53 us

profile of v5, /device:TPU:24, one launch (start us, length us, event | category | flops | bytes accessed | tf_op | source)
XLA Modules:
  0.0 126.5 jit_solution(6296853850756171679)
XLA Ops:
  0.0 0.0 copy-start.2
  0.0 0.0 copy-start.1
  0.0 0.7 copy-done.2
  0.7 0.0 copy-start.3
  0.7 0.7 pad_select_fusion.o_in
  1.4 0.0 copy-done.3
  1.4 0.7 copy.13.owner_col
  2.1 0.0 copy-done.1
  2.1 0.1 reshape.6
  2.2 0.1 reshape.8
  2.3 0.0 copy-start
  2.3 0.6 pad.16.q_in
  2.9 0.2 copy-done
  3.1 0.6 pad.19.m_in
  3.7 120.8 %shard_map.82 = bf16[256,1280]{1,0:T(8,128)(2,1)} custom-call(bf16[128,1280]{1,0:T(8,128)(2,1)} %tok_in.1, f32[2,1280]{1,0:T(2,128)} %gain_in.1, bf16[2,16,512]{2,1,0:T(8,128)(2,1)} %pad.16.q_in, bf16[16,384]{1,0:T(8,128)(2,1)} %pad_select_fusion.o_in, bf16[16,1280]{1,0:T(8,128)(2,1)} %pad.19.m_in, s32[1,128]{1,0:T(1,128)} %seg_row.1, s32[1,128]{1,0:T(1,128)} %order_row.1, ...), custom_call_target="tpu_custom_call" | custom-call | tf_op jit(solution)/shard_map/pallas_call | solution.py:564
  124.5 2.0 %copy.17 = bf16[256,1280]{1,0:T(8,128)(2,1)} copy(bf16[256,1280]{1,0:T(8,128)(2,1)} %shard_map.82) | data formatting | bytes 1310720
  (1 shorter events, 0.0 us)
Async XLA Ops:
  0.0 0.7 copy-start.2
  0.0 2.1 %copy-start.1 = (bf16[3,10,320]{2,0,1:T(4,128)(2,1)S(1)}, bf16[3,10,320]{2,0,1:T(4,128)(2,1)}, u32[]{:S(2)}) copy-start(bf16[3,10,320]{2,0,1:T(4,128)(2,1)} %param.9) | copy-start | bytes 57604
  0.7 0.7 copy-start.3
  2.3 0.8 copy-start

commit v6 on v5

--- a/solution.py
+++ b/solution.py
@@ -316,7 +316,8 @@
     for step in range(1, 9):
         serve(step)
         spread_out(step)
-        pass_on(step - 1)
+        if step > 1:
+            pass_on(step - 2)
         if step == 4:
             for dx in (1, 3):
                 n_copy(dx, False).wait_recv()
@@ -369,6 +370,7 @@
     att_in[rows_of(fs * 2 + xh, 160), :] = att_out[member]
     for step in range(1, 4):
         a_copy(step, True).start()
+    pass_on(7)
     pass_on(8)
     for step in range(1, 8):
         a_copy(step, False).wait_recv()

time: 128 us -> 127 us (level)
  Pallas kernels: 121 us -> 119 us
    pallas_call x1, Pallas kernels: 121 us -> 119 us  [block(): pl.pallas_call(block_kernel, out_shape=jax.ShapeDtypeStruct((256, 1280),...]
where the time goes in v6:
time: 127 us; the launch traced here: 125 us
  Pallas kernels  119 us (94%)
  local copies, waits for them, and re-layouts  4.98 us (4%)
    pallas_call x1, Pallas kernels, block(): pl.pallas_call(block_kernel, out_shape=jax.ShapeDtypeStruct((256, 1280),...  119 us
    unnamed x10, local copies, waits for them, and re-layouts  3.53 us

profile of v6, /device:TPU:24, one launch (start us, length us, event | category | flops | bytes accessed | tf_op | source)
XLA Modules:
  0.0 124.7 jit_solution(13487592400195506131)
XLA Ops:
  0.0 0.0 copy-start.2
  0.0 0.0 copy-start.1
  0.0 0.7 copy-done.2
  0.7 0.0 copy-start.3
  0.7 0.7 pad_select_fusion.o_in
  1.4 0.0 copy-done.3
  1.4 0.7 copy.13.owner_col
  2.1 0.0 copy-done.1
  2.1 0.1 reshape.6
  2.2 0.1 reshape.8
  2.3 0.0 copy-start
  2.3 0.6 pad.16.q_in
  2.9 0.2 copy-done
  3.1 0.6 pad.19.m_in
  3.7 119.0 %shard_map.82 = bf16[256,1280]{1,0:T(8,128)(2,1)} custom-call(bf16[128,1280]{1,0:T(8,128)(2,1)} %tok_in.1, f32[2,1280]{1,0:T(2,128)} %gain_in.1, bf16[2,16,512]{2,1,0:T(8,128)(2,1)} %pad.16.q_in, bf16[16,384]{1,0:T(8,128)(2,1)} %pad_select_fusion.o_in, bf16[16,1280]{1,0:T(8,128)(2,1)} %pad.19.m_in, s32[1,128]{1,0:T(1,128)} %seg_row.1, s32[1,128]{1,0:T(1,128)} %order_row.1, ...), custom_call_target="tpu_custom_call" | custom-call | tf_op jit(solution)/shard_map/pallas_call | solution.py:566
  122.7 2.0 %copy.17 = bf16[256,1280]{1,0:T(8,128)(2,1)} copy(bf16[256,1280]{1,0:T(8,128)(2,1)} %shard_map.82) | data formatting | bytes 1310720
  (1 shorter events, 0.0 us)
Async XLA Ops:
  0.0 0.7 copy-start.2
  0.0 2.1 %copy-start.1 = (bf16[3,10,320]{2,0,1:T(4,128)(2,1)S(1)}, bf16[3,10,320]{2,0,1:T(4,128)(2,1)}, u32[]{:S(2)}) copy-start(bf16[3,10,320]{2,0,1:T(4,128)(2,1)} %param.9) | copy-start | bytes 57604
  0.7 0.7 copy-start.3
  2.3 0.8 copy-start

commit v7 on v6

--- a/solution.py
+++ b/solution.py
@@ -44,6 +44,7 @@
     tok_in, gain_in, q_in, o_in, m_in, seg_row, order_row, owner_col, out, seg_in,
     wq, wo, wm, unmove, tok_t, normed_all, seg_all, q_box, o_box, m_box, slots,
     qkv, att_out, att_in, mi_out, mi_in, part_out, part_in, rows, picked1, picked2, picked3, landed1, landed2, landed3,
+    part_f, pair_out, pair_in, t_send, t_recv,
     c_send, c_recv, y_send, y_recv, e_send, e_recv,
     q_send, q_recv, o_send, o_recv, m_send, m_recv, n_send, n_recv, g_send, g_recv,
     s_send, s_recv, a_send, a_recv, i_send, i_recv, r_send, r_recv, p_send, p_recv,
@@ -407,23 +408,28 @@
     for step in range(1, 8):
         i_copy(step, False).wait_recv()
 
-    def r_copy(c, step, to):
-        dx, df = step // 4, step % 4
-        oxh = (xh + dx) % 2
-        ofs = (fs + df) % 4 if to else (fs + 4 - df) % 4
-        other = oxh * 4 + ofs
-        slot = member if to else other
-        return copy(
-            part_out.at[c, other], part_in.at[c, slot], r_send.at[c, step], r_recv.at[c, step], dev(oxh, y, z, ofs)
-        )
+    def t_copy(c):
+        return copy(pair_out.at[c], pair_in.at[c], t_send.at[c], t_recv.at[c], sibling)
+
+    def r_copy(c, dx, to):
+        other = (spot + dx) % 4 if to else (spot + 4 - dx) % 4
+        slot = spot if to else other
+        there = dev(other // 2, y, z, other % 2 * 2 + core)
+        return copy(part_out.at[c, other], part_in.at[c, slot], r_send.at[c, dx], r_recv.at[c, dx], there)
 
     inputs = mi_in[...].reshape(256, 640)
     for c in range(CH):
-        part = mix(inputs, wm[:, :, c * CW : (c + 1) * CW].reshape(640, CW)).astype(bf)
-        part_out[c] = part.reshape(8, 32, CW)
-        for step in range(1, 8):
-            r_copy(c, step, True).start()
-        part_in[c, member] = part_out[c, member]
+        part_f[c] = mix(inputs, wm[:, :, c * CW : (c + 1) * CW].reshape(640, CW)).reshape(4, 2, 32, CW)
+        for s in range(4):
+            pair_out[c, s] = part_f[c, s, 1 - core].astype(bf)
+        t_copy(c).start()
+    for c in range(CH):
+        t_copy(c).wait_recv()
+        for s in range(4):
+            part_out[c, s] = (part_f[c, s, core] + pair_in[c, s].astype(jnp.float32)).astype(bf)
+        for dx in (2, 1, 3):
+            r_copy(c, dx, True).start()
+        part_in[c, spot] = part_out[c, spot]
 
     def seat(way, gone):
         return 0 if gone == 0 else 15 if gone == 8 else 2 * gone - 1 + way
@@ -435,8 +441,8 @@
         )
 
     for c in range(CH):
-        for step in range(1, 8):
-            r_copy(c, step, False).wait_recv()
+        for dx in range(1, 4):
+            r_copy(c, dx, False).wait_recv()
         rows[c, 0] = jnp.sum(part_in[c].astype(jnp.float32), axis=0).astype(bf)
         for way in range(2):
             e_copy(c, way, 1).start()
@@ -521,9 +527,12 @@
         a_copy(step, True).wait_send()
         i_copy(step, True).wait_send()
         for c in range(CH):
-            r_copy(c, step, True).wait_send()
             for part in range(3):
                 p_copy(part, c, step, True).wait_send()
+    for c in range(CH):
+        t_copy(c).wait_send()
+        for dx in range(1, 4):
+            r_copy(c, dx, True).wait_send()
     for dx in range(4):
         n_share(dx, True).wait_send()
         if dx:
@@ -573,8 +582,9 @@
             vm((1280, 128), bf), vm((8, 128, 1280), bf), vm((8, 8, 128), jnp.int32),
             vm((8, 16, 512), bf), vm((2, 8, 16, 384), bf), vm((2, 4, 16, 256), bf), vm((NZ, 8, 128), jnp.int32),
             vm((512, 512), bf), vm((8, 160, 128), bf), vm((1280, 128), bf), vm((8, 32, 640), bf), vm((8, 32, 640), bf),
-            vm((CH, 8, 32, CW), bf), vm((CH, 8, 32, CW), bf), vm((CH, NZ, 32, CW), bf),
+            vm((CH, 4, 32, CW), bf), vm((CH, 4, 32, CW), bf), vm((CH, NZ, 32, CW), bf),
             vm((CH, 8, 16, CW), bf), vm((CH, 8, 8, CW), bf), vm((CH, 8, 8, CW), bf), vm((CH, 8, 16, CW), bf), vm((CH, 8, 8, CW), bf), vm((CH, 8, 8, CW), bf),
+            vm((CH, 4, 2, 32, CW), jnp.float32), vm((CH, 4, 32, CW), bf), vm((CH, 4, 32, CW), bf), dma((CH,)), dma((CH,)),
             dma((6, 2, 8)), dma((6, 2, 8)), dma((17, 6)), dma((17, 6)), dma((CH, 2, 8)), dma((CH, 2, 8)),
             dma((8,)), dma((8,)), dma((16,)), dma((2, 16)), dma((2, 4)), dma((2, 4)),
             dma((8,)), dma((8,)), dma((8,)), dma((8,)),

time: 127 us -> 125 us (0.984)
    pallas_call x1, Pallas kernels: 119 us -> 118 us  [block(): pl.pallas_call(block_kernel, out_shape=jax.ShapeDtypeStruct((256, 1280),...]
where the time goes in v7:
time: 125 us; the launch traced here: 123 us
  Pallas kernels  118 us (94%)
  local copies, waits for them, and re-layouts  4.98 us (4%)
    pallas_call x1, Pallas kernels, block(): pl.pallas_call(block_kernel, out_shape=jax.ShapeDtypeStruct((256, 1280),...  118 us
    unnamed x10, local copies, waits for them, and re-layouts  3.53 us

profile of v7, /device:TPU:24, one launch (start us, length us, event | category | flops | bytes accessed | tf_op | source)
XLA Modules:
  0.0 123.3 jit_solution(6488559269468251936)
XLA Ops:
  0.0 0.0 copy-start.2
  0.0 0.0 copy-start.1
  0.0 0.7 copy-done.2
  0.7 0.0 copy-start.3
  0.7 0.7 pad_select_fusion.o_in
  1.4 0.0 copy-done.3
  1.4 0.7 copy.13.owner_col
  2.1 0.0 copy-done.1
  2.1 0.1 reshape.6
  2.2 0.1 reshape.8
  2.3 0.0 copy-start
  2.3 0.6 pad.16.q_in
  2.9 0.2 copy-done
  3.1 0.6 pad.19.m_in
  3.7 117.6 %shard_map.82 = bf16[256,1280]{1,0:T(8,128)(2,1)} custom-call(bf16[128,1280]{1,0:T(8,128)(2,1)} %tok_in.1, f32[2,1280]{1,0:T(2,128)} %gain_in.1, bf16[2,16,512]{2,1,0:T(8,128)(2,1)} %pad.16.q_in, bf16[16,384]{1,0:T(8,128)(2,1)} %pad_select_fusion.o_in, bf16[16,1280]{1,0:T(8,128)(2,1)} %pad.19.m_in, s32[1,128]{1,0:T(1,128)} %seg_row.1, s32[1,128]{1,0:T(1,128)} %order_row.1, ...), custom_call_target="tpu_custom_call" | custom-call | tf_op jit(solution)/shard_map/pallas_call | solution.py:575
  121.3 2.0 %copy.17 = bf16[256,1280]{1,0:T(8,128)(2,1)} copy(bf16[256,1280]{1,0:T(8,128)(2,1)} %shard_map.82) | data formatting | bytes 1310720
  (1 shorter events, 0.0 us)
Async XLA Ops:
  0.0 0.7 copy-start.2
  0.0 2.1 %copy-start.1 = (bf16[3,10,320]{2,0,1:T(4,128)(2,1)S(1)}, bf16[3,10,320]{2,0,1:T(4,128)(2,1)}, u32[]{:S(2)}) copy-start(bf16[3,10,320]{2,0,1:T(4,128)(2,1)} %param.9) | copy-start | bytes 57604
  0.7 0.7 copy-start.3
  2.3 0.8 copy-start
